TPU v7x, 512 devices: a whole 4x8x8 slice. The times are simulated.
512 devices in a mesh: dp: 2 (over x_lo), row: 16 (over x_hi, y), col: 16 (over z, core).
Axes of the slice: x: 4 (x_hi: 2, x_lo: 2; x = x_hi * 2 + x_lo), y: 8, z: 8, core: 2. Of those that a mesh axis runs over, the one named last changes fastest.
Arguments:
- tokens: bfloat16 [320, 8192], P('dp', 'row'), may hold values from -6 to 6
- cotangent: bfloat16 [320, 8192], P('dp', 'row'), may hold values from -6 to 6
- up_weight: bfloat16 [8192, 28672], P('row', ('dp', 'col')), may hold values from -0.0625 to 0.0625
- down_weight: bfloat16 [28672, 8192], P(('dp', 'col'), 'row'), may hold values from -0.03125 to 0.03125
Outputs:
- output: bfloat16 [320, 8192], P(('dp', 'col'), 'row')
- input_grad: bfloat16 [320, 8192], P(('dp', 'col'), 'row')
- up_grad: bfloat16 [8192, 28672], P('row', ('dp', 'col'))
- down_grad: bfloat16 [28672, 8192], P(('dp', 'col'), 'row')
All inputs are finite; a program needn't handle non-finite values.
Results may differ from a plain program's by a relative error of at most 0.0061.
Values may be sent and summed in bfloat16 or wider, within the bound.
No kernel may reach another device: no remote copies, remote signals or barrier semaphores. Data moves between devices by JAX's collectives and lax.ppermute only.
A program may use at most 64 MiB of HBM per device.

v0:
```python
import jax
import jax.numpy as jnp
from jax import lax
from jax.sharding import PartitionSpec as P


def silu_slope(pre_wide):
    sigma = jax.nn.sigmoid(pre_wide)
    return sigma * (1.0 + pre_wide * (1.0 - sigma))


def widen(values):
    return lax.optimization_barrier(values.astype(jnp.bfloat16)).astype(jnp.float32)


def body(tokens, cotangent, up_weight, down_weight):
    pair_acts, pair_cots = (
        lax.all_gather(tokens, "dp", axis=0, tiled=True),
        lax.all_gather(cotangent, "dp", axis=0, tiled=True),
    )
    up_part = jnp.dot(pair_acts, up_weight, preferred_element_type=jnp.float32)
    back_part = lax.dot_general(
        pair_cots, down_weight, (((1,), (1,)), ((), ())), preferred_element_type=jnp.float32
    )
    pre_wide = widen(lax.psum(up_part, "row"))
    hidden = jax.nn.silu(pre_wide).astype(jnp.bfloat16)
    grad_hidden = widen(lax.psum(back_part, "row"))
    grad_pre = (grad_hidden * silu_slope(pre_wide)).astype(jnp.bfloat16)
    picked = hidden
    output = lax.psum_scatter(
        jnp.dot(picked, down_weight, preferred_element_type=jnp.float32),
        ("dp", "col"),
        scatter_dimension=0,
        tiled=True,
    ).astype(jnp.bfloat16)
    picked = grad_pre
    input_grad = lax.psum_scatter(
        lax.dot_general(
            picked, up_weight, (((1,), (1,)), ((), ())), preferred_element_type=jnp.float32
        ),
        ("dp", "col"),
        scatter_dimension=0,
        tiled=True,
    ).astype(jnp.bfloat16)
    up_grad = lax.dot_general(
        pair_acts, grad_pre, (((0,), (0,)), ((), ())), preferred_element_type=jnp.float32
    ).astype(jnp.bfloat16)
    down_grad = lax.dot_general(
        hidden, pair_cots, (((0,), (0,)), ((), ())), preferred_element_type=jnp.float32
    ).astype(jnp.bfloat16)
    return (output, input_grad, up_grad, down_grad)


def solution(mesh):
    return jax.shard_map(
        body,
        mesh=mesh,
        in_specs=(P("dp", "row"), P("dp", "row"), P("row", ("dp", "col")), P(("dp", "col"), "row")),
        out_specs=(
            P(("dp", "col"), "row"),
            P(("dp", "col"), "row"),
            P("row", ("dp", "col")),
            P(("dp", "col"), "row"),
        ),
        check_vma=False,
    )
```

profile of v0, /device:TPU:2, one launch (start us, length us, event | category | flops | bytes accessed | tf_op | source)
XLA Modules:
  0.0 246.7 jit_solution(5781469683513583128)
XLA Ops:
  0.6 0.0 copy-start
  0.6 11.2 %all_gather.6 = bf16[320,512]{1,0:T(8,128)(2,1)S(1)} all-gather(bf16[160,512]{1,0:T(8,128)(2,1)} %param.4), channel_id=1, replica_groups=mesh['dp'=2,'row'=16,'col'=16] {'dp'}, dimensions={0}, use_global_device_ids=true | all-gather | bytes 491520 | tf_op jit(solution)/shard_map/all_gather | solution.py:18
  11.9 0.0 copy-done
  11.9 0.0 copy-start.1
  11.9 0.0 copy-start.7
  11.9 0.0 copy-start.3
  11.9 0.5 fusion.12
  12.4 0.2 copy-done.1
  12.6 0.3 copy-done.7
  12.9 6.0 %all_gather.7 = bf16[320,512]{1,0:T(8,128)(2,1)S(1)} all-gather(bf16[160,512]{1,0:T(8,128)(2,1)S(1)} %copy-done.7), channel_id=1, replica_groups=mesh['dp'=2,'row'=16,'col'=16] {'dp'}, dimensions={0}, use_global_device_ids=true | all-gather | bytes 491520 | tf_op jit(solution)/shard_map/all_gather | solution.py:19
  18.9 0.0 copy-done.3
  18.9 0.5 fusion.13
  19.4 92.3 %all-reduce.6 = (bf16[320,896]{1,0:T(8,128)(2,1)}, bf16[320,896]{1,0:T(8,128)(2,1)}) all-reduce(f32[320,896]{1,0:T(8,128)S(1)} %fusion.12, f32[320,896]{1,0:T(8,128)S(1)} %fusion.13), channel_id=1, replica_groups=mesh['dp'=2,'row'=16,'col'=16] {'row'}, use_global_device_ids=true, to_apply=%region_0.0 | all-reduce | flops 573440 | bytes 3440640 | tf_op jit(solution)/shard_map/psum | solution.py:25
  111.7 1.7 fusion.8
  113.4 0.0 copy-start.4
  113.4 0.0 copy-start.5
  113.4 0.5 fusion.14
  114.0 0.6 copy-done.4
  114.6 0.2 copy-done.5
  114.8 1.4 fusion.10
  116.1 0.0 copy-start.2
  116.1 122.5 %all-reduce.7 = (bf16[320,512]{1,0:T(8,128)(2,1)S(1)}, bf16[320,512]{1,0:T(8,128)(2,1)S(1)}) all-reduce(f32[320,512]{1,0:T(8,128)} %fusion.10, f32[320,512]{1,0:T(8,128)S(1)} %fusion.14), channel_id=2, replica_groups=mesh['dp'=2,'row'=16,'col'=16] {'dp','col'}, use_global_device_ids=true, to_apply=%region_1.2.clone | all-reduce | flops 327680 | bytes 1966080
  238.7 1.3 dynamic-slice
  240.6 0.6 dynamic-slice_convert_fusion
  241.2 0.0 copy-done.2
  241.2 1.6 fusion
  242.8 0.0 copy-start.6
  242.8 2.3 copy.9
  245.1 0.0 copy-done.6
  245.1 1.6 convolution_convert_fusion
Async XLA Ops:
  0.6 11.3 %copy-start = (bf16[512,896]{1,0:T(8,128)(2,1)S(1)}, bf16[512,896]{1,0:T(8,128)(2,1)}, u32[]{:S(2)}) copy-start(bf16[512,896]{1,0:T(8,128)(2,1)} %param.6) | copy-start | bytes 2752516
  11.9 0.7 copy-start.1
  11.9 1.0 copy-start.7
  11.9 7.0 %copy-start.3 = (bf16[896,512]{1,0:T(8,128)(2,1)S(1)}, bf16[896,512]{1,0:T(8,128)(2,1)}, u32[]{:S(2)}) copy-start(bf16[896,512]{1,0:T(8,128)(2,1)} %param.7) | copy-start | bytes 2752516
  113.4 1.2 copy-start.4
  113.4 1.3 copy-start.5
  116.1 125.1 %copy-start.2 = (bf16[320,512]{1,0:T(8,128)(2,1)S(1)}, bf16[320,512]{1,0:T(8,128)(2,1)}, u32[]{:S(2)}) copy-start(bf16[320,512]{1,0:T(8,128)(2,1)} %copy-done.1) | copy-start | bytes 983044
  242.8 2.3 copy-start.6
where the time goes:
time: 247 us
  blocking collectives  232 us (94%)
  matrix products  6.17 us (2%)
  local copies, waits for them, and re-layouts  5.48 us (2%)
    unnamed x1, blocking collectives  123 us
    psum x1, blocking collectives, body(): pre_wide = widen(lax.psum(up_part, 'row'))  92.3 us
    all_gather x1, blocking collectives, body(): lax.all_gather(tokens, 'dp', axis=0, tiled=True)  11.2 us
    all_gather x1, blocking collectives, body(): lax.all_gather(cotangent, 'dp', axis=0, tiled=True)  5.98 us

commit v1 on v0

v1 whole, which is shorter than its diff:
```python
import jax
import jax.numpy as jnp
from jax import lax
from jax.sharding import Mesh, PartitionSpec as P

ROW = ("xh", "y")
f32, bf16 = jnp.float32, jnp.bfloat16


def silu_slope(pre_wide):
    sigma = jax.nn.sigmoid(pre_wide)
    return sigma * (1.0 + pre_wide * (1.0 - sigma))


def dot(a, b, dims):
    return lax.dot_general(a, b, (dims, ((), ())), preferred_element_type=f32)


def body(tokens, cotangent, up_weight, down_weight):
    both = lax.all_gather(jnp.stack([tokens, cotangent]), "dp", axis=1, tiled=True)
    acts, cots = both[0], both[1]
    count, hid = acts.shape[0], up_weight.shape[1]
    width = acts.shape[1]
    rows = count // 16
    up_part = dot(acts, up_weight, ((1,), (0,))).astype(bf16)
    back_part = dot(cots, down_weight, ((1,), (1,))).astype(bf16)
    parts = jnp.concatenate([up_part.reshape(16, rows, hid), back_part.reshape(16, rows, hid)], axis=1)
    parts = lax.all_to_all(parts, ROW, 0, 0, tiled=True)
    sums = jnp.sum(parts.astype(f32), axis=0).astype(bf16)
    pre_wide = sums[:rows].astype(f32)
    hidden = jax.nn.silu(pre_wide).astype(bf16)
    grad_pre = (sums[rows:].astype(f32) * silu_slope(pre_wide)).astype(bf16)
    mine = jnp.concatenate([hidden, grad_pre], axis=0)
    full = lax.all_to_all(jnp.broadcast_to(mine, (16,) + mine.shape), ROW, 0, 0, tiled=True)
    hidden = full[:, :rows].reshape(count, hid)
    grad_pre = full[:, rows:].reshape(count, hid)
    out_part = dot(hidden, down_weight, ((1,), (0,))).astype(bf16)
    in_part = dot(grad_pre, up_weight, ((1,), (1,))).astype(bf16)
    mini = count // 32
    parts = jnp.stack([out_part.reshape(16, 2, mini, width), in_part.reshape(16, 2, mini, width)], axis=2)
    parts = jnp.moveaxis(parts, 1, 0)
    parts = lax.all_to_all(parts, "c", 0, 0, tiled=True)
    parts = jnp.sum(parts.astype(f32), axis=0).astype(bf16)
    parts = lax.all_to_all(parts, ("dp", "z"), 0, 0, tiled=True)
    sums = jnp.sum(parts.astype(f32), axis=0).astype(bf16)
    up_grad = dot(acts, grad_pre, ((0,), (0,))).astype(bf16)
    down_grad = dot(hidden, cots, ((0,), (0,))).astype(bf16)
    return sums[0], sums[1], up_grad, down_grad


def solution(mesh):
    fine = Mesh(mesh.devices.reshape(2, 2, 8, 8, 2), ("dp", "xh", "y", "z", "c"))
    split = ("dp", "z", "c")
    acts, up, down = P("dp", ROW), P(ROW, split), P(split, ROW)
    return jax.shard_map(
        body,
        mesh=fine,
        in_specs=(acts, acts, up, down),
        out_specs=(down, down, up, down),
        check_vma=False,
    )
```

time: 247 us -> 125 us (0.51)
  the two profiles are of different devices: /device:TPU:2 before, /device:TPU:56 now
where the time goes in v1:
time: 125 us; the launch traced here: 122 us
  blocking collectives  86.7 us (69%)
  starting transfers between devices  10.5 us (8%)
  waiting for transfers between devices  8.41 us (7%)
  matrix products  8.11 us (6%)
  local copies, waits for them, and re-layouts  5.81 us (5%)
  other arithmetic  2.18 us (2%)
    all_to_all x1, blocking collectives, body(): parts = lax.all_to_all(parts, ROW, 0, 0, tiled=True)  38.5 us
    all_to_all x1, blocking collectives, body(): lax.all_to_all(jnp.broadcast_to(mine, (16,) + mine.shape), ROW, 0, 0, til...  33.8 us
    all_to_all x1, starting transfers between devices, body(): parts = lax.all_to_all(parts, ('dp', 'z'), 0, 0, tiled=True)  10.5 us
    all_gather x1, blocking collectives, body(): lax.all_gather(jnp.stack([tokens, cotangent]), 'dp', axis=1, tiled=True)  10.1 us
    all_to_all x1, waiting for transfers between devices, body(): parts = lax.all_to_all(parts, ('dp', 'z'), 0, 0, tiled=True)  8.41 us
    dot_general x6, matrix products, dot(): return lax.dot_general(a, b, (dims, ((), ())), preferred_element_type=f32)  8.11 us
    all_to_all x1, blocking collectives, body(): parts = lax.all_to_all(parts, 'c', 0, 0, tiled=True)  4.26 us
  transfers between devices with their start and end apart: 1, of which 1 were waited for; matrix products, arithmetic and copies ran while one was open for 3% of the time, Pallas kernels for 0%

profile of v1, /device:TPU:56, one launch (start us, length us, event | category | flops | bytes accessed | tf_op | source)
XLA Modules:
  0.0 122.4 jit_solution(10693499426977848731)
XLA Ops:
  0.6 0.0 copy-start
  0.6 0.0 copy-start.1
  0.7 1.2 pad_maximum_fusion.1
  1.8 10.1 %all_gather.3 = bf16[2,320,512]{2,1,0:T(8,128)(2,1)S(1)} all-gather(bf16[2,160,512]{2,1,0:T(8,128)(2,1)S(1)} %pad_maximum_fusion.1), channel_id=1, replica_groups=mesh['dp'=2,'xh'=2,'y'=8,'z'=8,'c'=2] {'dp'}, dimensions={1}, use_global_device_ids=true | all-gather | bytes 983040 | tf_op jit(solution)/shard_map/all_gather | solution.py:20
  11.9 0.0 copy-done.1
  11.9 0.5 convolution_convert_fusion.3
  12.5 0.1 reshape.20
  12.6 0.0 copy-done
  12.6 0.5 convolution_convert_fusion.2
  13.1 0.1 reshape.21
  13.3 0.2 pad_maximum_fusion
  13.5 38.5 %all_to_all.20 = bf16[16,40,896]{2,1,0:T(8,128)(2,1)S(1)} all-to-all(bf16[16,40,896]{2,1,0:T(8,128)(2,1)S(1)} %pad_maximum_fusion), channel_id=1, replica_groups=mesh['dp'=2,'xh'=2,'y'=8,'z'=8,'c'=2] {'xh','y'}, dimensions={0} | all-to-all | bytes 2293760 | tf_op jit(solution)/shard_map/all_to_all | solution.py:28
  52.0 0.2 reduce_sum.36
  52.2 0.1 fusion.3
  52.3 0.1 broadcast_in_dim.3
  52.4 33.8 %all_to_all.21 = bf16[16,40,896]{2,1,0:T(8,128)(2,1)S(1)} all-to-all(bf16[16,40,896]{2,1,0:T(8,128)(2,1)S(1)} %broadcast_in_dim.3), channel_id=1, replica_groups=mesh['dp'=2,'xh'=2,'y'=8,'z'=8,'c'=2] {'xh','y'}, dimensions={0} | all-to-all | bytes 2293760 | tf_op jit(solution)/shard_map/all_to_all | solution.py:34
  86.1 0.2 fusion.8
  86.3 0.1 reshape.22
  86.5 1.2 %convolution_convert_fusion.5 = bf16[320,512]{1,0:T(8,128)(2,1)} fusion(bf16[320,896]{1,0:T(8,128)(2,1)S(1)} %reshape.22, bf16[896,512]{1,0:T(8,128)(2,1)S(1)} %copy-done), kind=kOutput, calls=%fused_computation.5 | convolution fusion | flops 293765120 | bytes 1818624 | tf_op jit(solution)/shard_map/dot_general | solution.py:16
  87.7 1.1 stack_reshape.6
  88.8 0.9 reshape.23
  89.7 2.6 %convolution_convert_fusion.4 = bf16[320,512]{1,0:T(8,128)(2,1)} fusion(bf16[320,896]{1,0:T(8,128)(2,1)} %reshape.23, bf16[512,896]{1,0:T(8,128)(2,1)} %param.6), kind=kOutput, calls=%fused_computation.4 | convolution fusion | flops 293765120 | bytes 1818624 | tf_op jit(solution)/shard_map/dot_general | solution.py:16
  92.3 1.1 stack_reshape.7
  93.4 0.1 maximum_bitcast_fusion
  93.5 0.4 copy.14
  93.9 4.3 %all_to_all.22 = bf16[2,16,2,10,512]{4,1,3,2,0:T(8,128)(2,1)S(1)} all-to-all(bf16[2,16,2,10,512]{4,1,3,2,0:T(8,128)(2,1)S(1)} %copy.14), channel_id=1, replica_groups=mesh['dp'=2,'xh'=2,'y'=8,'z'=8,'c'=2] {'c'}, dimensions={0} | all-to-all | bytes 1310720 | tf_op jit(solution)/shard_map/all_to_all | solution.py:42
  98.2 0.1 reduce_sum.37
  98.3 1.0 copy.16
  99.4 10.5 %all-to-all-start.3 = ((bf16[16,2,10,512]{3,1,2,0:T(2,128)(2,1)}), bf16[16,2,10,512]{3,1,2,0:T(2,128)(2,1)S(1)}, u32[]{:S(2)}, u32[]{:S(2)}) async-start(bf16[16,2,10,512]{3,1,2,0:T(2,128)(2,1)} %copy.16), calls=%async_computation.3 | async-start | bytes 655360 | tf_op jit(solution)/shard_map/all_to_all | solution.py:44
  109.8 0.0 copy-start.2
  109.8 1.6 %convolution_convert_fusion = bf16[896,512]{1,0:T(8,128)(2,1)} fusion(bf16[320,896]{1,0:T(8,128)(2,1)S(1)} %reshape.22, bf16[2,320,512]{2,1,0:T(8,128)(2,1)S(1)} %all_gather.3), kind=kOutput, calls=%fused_computation | convolution fusion | flops 294060032 | bytes 1818624 | tf_op jit(solution)/shard_map/dot_general | solution.py:16
  111.4 0.0 copy-done.2
  111.4 1.6 %convolution_convert_fusion.1 = bf16[512,896]{1,0:T(8,128)(2,1)} fusion(bf16[320,896]{1,0:T(8,128)(2,1)S(1)} %copy-done.2, bf16[2,320,512]{2,1,0:T(8,128)(2,1)S(1)} %all_gather.3), kind=kOutput, calls=%fused_computation.1 | convolution fusion | flops 294060032 | bytes 1818624 | tf_op jit(solution)/shard_map/dot_general | solution.py:16
  113.1 8.4 %all-to-all-done.3 = bf16[16,2,10,512]{3,1,2,0:T(2,128)(2,1)S(1)} async-done(((bf16[16,2,10,512]{3,1,2,0:T(2,128)(2,1)}), bf16[16,2,10,512]{3,1,2,0:T(2,128)(2,1)S(1)}, u32[]{:S(2)}, u32[]{:S(2)}) %all-to-all-start.3) | async-done | bytes 327712 | tf_op jit(solution)/shard_map/all_to_all | solution.py:44
  121.5 0.3 reduce_sum.38
  121.8 0.6 copy_bitcast_fusion
  (2 shorter events, 0.1 us)
Async XLA Ops:
  0.6 12.0 %copy-start = (bf16[896,512]{1,0:T(8,128)(2,1)S(1)}, bf16[896,512]{1,0:T(8,128)(2,1)}, u32[]{:S(2)}) copy-start(bf16[896,512]{1,0:T(8,128)(2,1)} %param.7) | copy-start | bytes 2752516
  0.6 11.3 %copy-start.1 = (bf16[512,896]{1,0:T(8,128)(2,1)S(1)}, bf16[512,896]{1,0:T(8,128)(2,1)}, u32[]{:S(2)}) copy-start(bf16[512,896]{1,0:T(8,128)(2,1)} %param.6) | copy-start | bytes 2752516
  99.4 22.1 %all-to-all-start.3 = ((bf16[16,2,10,512]{3,1,2,0:T(2,128)(2,1)}), bf16[16,2,10,512]{3,1,2,0:T(2,128)(2,1)S(1)}, u32[]{:S(2)}, u32[]{:S(2)}) async-start(bf16[16,2,10,512]{3,1,2,0:T(2,128)(2,1)} %copy.16), calls=%async_computation.3 | async-start | bytes 655360 | tf_op jit(solution)/shard_map/all_to_all | solution.py:44
  109.8 1.6 %copy-start.2 = (bf16[320,896]{1,0:T(8,128)(2,1)S(1)}, bf16[320,896]{1,0:T(8,128)(2,1)}, u32[]{:S(2)}) copy-start(bf16[320,896]{1,0:T(8,128)(2,1)} %reshape.23) | copy-start | bytes 1720324

commit v2 on v1

v2 whole, which is shorter than its diff:
```python
import jax
import jax.numpy as jnp
from jax import lax
from jax.sharding import Mesh, PartitionSpec as P

ROW = ("xh", "y")
f32, bf16 = jnp.float32, jnp.bfloat16


def silu_slope(pre_wide):
    sigma = jax.nn.sigmoid(pre_wide)
    return sigma * (1.0 + pre_wide * (1.0 - sigma))


def dot(a, b, dims):
    return lax.dot_general(a, b, (dims, ((), ())), preferred_element_type=f32)


def add_up(parts):
    terms = [parts[i].astype(f32) for i in range(parts.shape[0])]
    while len(terms) > 1:
        terms = [a + b for a, b in zip(terms[::2], terms[1::2])]
    return terms[0]


def pick(first, low, high):
    return jnp.where(first, low, high), jnp.where(first, high, low)


def partials(acts, cots, up_weight, down_weight):
    rows = acts.shape[0] // 16
    up_part = dot(acts, up_weight, ((1,), (0,))).astype(bf16)
    back_part = dot(cots, down_weight, ((1,), (1,))).astype(bf16)
    return jnp.concatenate([up_part.reshape(16, rows, -1), back_part.reshape(16, rows, -1)], axis=1)


def activate(sums):
    rows = sums.shape[0] // 2
    sums = sums.astype(bf16).astype(f32)
    pre_wide = sums[:rows]
    hidden = jax.nn.silu(pre_wide).astype(bf16)
    grad_pre = (sums[rows:] * silu_slope(pre_wide)).astype(bf16)
    return jnp.concatenate([hidden, grad_pre], axis=0)


def unpack(full):
    rows = full.shape[1] // 2
    return full[:, :rows].reshape(-1, full.shape[2]), full[:, rows:].reshape(-1, full.shape[2])


def trade(parts, axis):
    return lax.all_to_all(parts, axis, 0, 0, tiled=True)


def copies(mine, count):
    return jnp.broadcast_to(mine, (count,) + mine.shape)


def body(tokens, cotangent, up_weight, down_weight):
    swap = [(0, 1), (1, 0)]
    at_dp, at_x, at_c = (lax.axis_index(n) == 0 for n in ("dp", "xh", "c"))
    far_acts = lax.ppermute(tokens, "dp", swap)
    far_cots = lax.ppermute(cotangent, "dp", swap)
    near = trade(partials(tokens, cotangent, up_weight, down_weight), ROW)
    far = partials(far_acts, far_cots, up_weight, down_weight)
    keep, send = pick(at_x, far[:8], far[8:])
    far = (keep.astype(f32) + lax.ppermute(send, "xh", swap).astype(f32)).astype(bf16)
    near, far = lax.optimization_barrier((near, far))
    far = trade(far, "y")
    near = activate(add_up(near))
    far = trade(copies(activate(add_up(far)), 8), "y")
    near, far = lax.optimization_barrier((near, far))
    other = lax.ppermute(far, "xh", swap)
    near = trade(copies(near, 16), ROW)
    far = jnp.concatenate(pick(at_x, far, other), axis=0)
    acts, cots = jnp.concatenate([tokens, far_acts]), jnp.concatenate([cotangent, far_cots])
    hidden, grad_pre = (jnp.concatenate(p) for p in zip(unpack(near), unpack(far)))
    out_part = dot(hidden, down_weight, ((1,), (0,))).astype(bf16)
    in_part = dot(grad_pre, up_weight, ((1,), (1,))).astype(bf16)
    ends = jnp.concatenate([out_part, in_part], axis=1)
    count, width = tokens.shape
    ends = jnp.concatenate(pick(at_dp, ends[:count], ends[count:]))
    ends = ends.reshape(16, 2, count // 16, 2 * width)
    keep, send = pick(at_c, ends[:, 0], ends[:, 1])
    ends = (keep.astype(f32) + lax.ppermute(send, "c", swap).astype(f32)).astype(bf16)
    sums = add_up(trade(ends, ("dp", "z"))).astype(bf16)
    up_grad = dot(acts, grad_pre, ((0,), (0,))).astype(bf16)
    down_grad = dot(hidden, cots, ((0,), (0,))).astype(bf16)
    return sums[:, :width], sums[:, width:], up_grad, down_grad


def solution(mesh):
    fine = Mesh(mesh.devices.reshape(2, 2, 8, 8, 2), ("dp", "xh", "y", "z", "c"))
    split = ("dp", "z", "c")
    acts, up, down = P("dp", ROW), P(ROW, split), P(split, ROW)
    return jax.shard_map(
        body,
        mesh=fine,
        in_specs=(acts, acts, up, down),
        out_specs=(down, down, up, down),
        check_vma=False,
    )
```

time: 125 us -> 138 us (1.10)
  blocking collectives: 86.7 us -> 16.3 us
  starting transfers between devices: 10.5 us -> 51.6 us
  waiting for transfers between devices: 8.41 us -> 44.5 us
  local copies, waits for them, and re-layouts: 5.81 us -> 8.63 us
  other arithmetic: 2.18 us -> 4.05 us
  matrix products: 8.11 us -> 9.76 us
    all_to_all x3 -> x1, blocking collectives: 76.5 us -> 16.3 us  [trade(): return lax.all_to_all(parts, axis, 0, 0, tiled=True)]
    ppermute x0 -> x5, waiting for transfers between devices: none -> 24.6 us  [the longest x1 11.9 us: body(): lax.ppermute(send, 'xh', swap).astype(f32)]
    all_to_all x1 -> x4, starting transfers between devices: 10.5 us -> 33.9 us  [trade(): return lax.all_to_all(parts, axis, 0, 0, tiled=True)]
    ppermute x0 -> x5, starting transfers between devices: none -> 17.7 us  [the longest x1 4.92 us: body(): other = lax.ppermute(far, 'xh', swap)]
    all_to_all x1 -> x4, waiting for transfers between devices: 8.41 us -> 19.8 us  [trade(): return lax.all_to_all(parts, axis, 0, 0, tiled=True)]
    all_gather x1 -> x0, blocking collectives: 10.1 us -> none  [body(): lax.all_gather(jnp.stack([tokens, cotangent]), 'dp', axis=1, tiled=True)]
    convert_element_type x1 -> x7, other arithmetic: 0.05 us -> 2.36 us  [the longest x1 1.09 us: body(): (keep.astype(f32) + lax.ppermute(send, 'c', swap).astype(f32)).astype(bf16)]
    another operation x2 -> x0, local copies, waits for them, and re-layouts: 2.16 us -> none  [body(): jnp.stack([out_part.reshape(16, 2, mini, width), in_part.reshape(16, 2, m...]
  transfers between devices with their start and end apart: 1 -> 9, of which waited for: 1 -> 5; matrix products, arithmetic and copies ran while one was open for 3% -> 10% of each run, Pallas kernels for 0% -> 0%
where the time goes in v2:
time: 138 us; the launch traced here: 136 us
  starting transfers between devices  51.6 us (37%)
  waiting for transfers between devices  44.5 us (32%)
  blocking collectives  16.3 us (12%)
  matrix products  9.76 us (7%)
  local copies, waits for them, and re-layouts  8.63 us (6%)
  other arithmetic  4.05 us (3%)
    all_to_all x4, starting transfers between devices, trade(): return lax.all_to_all(parts, axis, 0, 0, tiled=True)  33.9 us
    all_to_all x4, waiting for transfers between devices, trade(): return lax.all_to_all(parts, axis, 0, 0, tiled=True)  19.8 us
    all_to_all x1, blocking collectives, trade(): return lax.all_to_all(parts, axis, 0, 0, tiled=True)  16.3 us
    ppermute x1, waiting for transfers between devices, body(): lax.ppermute(send, 'xh', swap).astype(f32)  11.9 us
    ppermute x1, waiting for transfers between devices, body(): other = lax.ppermute(far, 'xh', swap)  10.8 us
    dot_general x8, matrix products, dot(): return lax.dot_general(a, b, (dims, ((), ())), preferred_element_type=f32)  9.76 us
    ppermute x1, starting transfers between devices, body(): other = lax.ppermute(far, 'xh', swap)  4.92 us
    ppermute x1, starting transfers between devices, body(): lax.ppermute(send, 'xh', swap).astype(f32)  4.88 us
  transfers between devices with their start and end apart: 9, of which 5 were waited for; matrix products, arithmetic and copies ran while one was open for 10% of the time, Pallas kernels for 0%

profile of v2, /device:TPU:56, one launch (start us, length us, event | category | flops | bytes accessed | tf_op | source)
XLA Modules:
  0.0 135.8 jit_solution(9780658151158146225)
XLA Ops:
  0.7 3.5 %collective-permute-start = (bf16[160,512]{1,0:T(8,128)(2,1)}, bf16[160,512]{1,0:T(8,128)(2,1)S(1)}, u32[]{:S(2)}, u32[]{:S(2)}) collective-permute-start(bf16[160,512]{1,0:T(8,128)(2,1)} %param.4), channel_id=1, source_target_pairs={{0,256},{256,0},{1,257},{257,1},{2,258},{258,2},{3,259},{259,3},{4... | collective-permute-start | bytes 491528 | tf_op jit(solution)/shard_map/ppermute | solution.py:62
  4.2 2.4 %collective-permute-start.1 = (bf16[160,512]{1,0:T(8,128)(2,1)}, bf16[160,512]{1,0:T(8,128)(2,1)}, u32[]{:S(2)}, u32[]{:S(2)}) collective-permute-start(bf16[160,512]{1,0:T(8,128)(2,1)} %param.5), channel_id=1, source_target_pairs={{0,256},{256,0},{1,257},{257,1},{2,258},{258,2},{3,259},{259,3},{4... | collective-permute-start | bytes 491528 | tf_op jit(solution)/shard_map/ppermute | solution.py:63
  6.7 1.6 %convolution_convert_fusion.7 = bf16[160,896]{1,0:T(8,128)(2,1)S(1)} fusion(bf16[160,512]{1,0:T(8,128)(2,1)} %param.4, bf16[512,896]{1,0:T(8,128)(2,1)} %param.6), kind=kOutput, calls=%fused_computation.7 | convolution fusion | flops 146944000 | bytes 1368064 | tf_op jit(solution)/shard_map/dot_general | solution.py:16
  8.3 0.5 convolution_convert_fusion.6
  8.8 0.1 reshape.117
  8.9 0.1 reshape.118
  9.0 1.0 pad_maximum_fusion
  10.0 9.5 %all-to-all-start = ((bf16[16,20,896]{2,1,0:T(8,128)(2,1)}), bf16[16,20,896]{2,1,0:T(8,128)(2,1)S(1)}, u32[]{:S(2)}, u32[]{:S(2)}) async-start(bf16[16,20,896]{2,1,0:T(8,128)(2,1)} %pad_maximum_fusion), calls=%async_computation | async-start | bytes 1376256 | tf_op jit(solution)/shard_map/all_to_all | solution.py:52
  19.5 0.7 copy-done.7
  20.1 0.3 convolution_convert_fusion.5
  20.5 0.1 reshape.119
  20.6 2.1 %convolution_convert_fusion.4 = bf16[160,896]{1,0:T(8,128)(2,1)} fusion(bf16[160,512]{1,0:T(8,128)(2,1)} %collective-permute-done.1, bf16[896,512]{1,0:T(8,128)(2,1)S(1)} %copy-done), kind=kOutput, calls=%fused_computation.4 | convolution fusion | flops 146944000 | bytes 1368064 | tf_op jit(solution)/shard_map/dot_general | solution.py:16
  22.7 1.1 reshape.120
  23.7 0.2 broadcast_select_fusion.2
  24.0 4.9 %collective-permute-start.2 = (bf16[8,20,896]{2,1,0:T(8,128)(2,1)S(1)}, bf16[8,20,896]{2,1,0:T(8,128)(2,1)S(1)}, u32[]{:S(2)}, u32[]{:S(2)}) collective-permute-start(bf16[8,20,896]{2,1,0:T(8,128)(2,1)S(1)} %broadcast_select_fusion.2), channel_id=1, source_target_pairs={{0,128},{128,0},{1,129},{129,1},{2,130},{130,2},{3,131},{131,3},{4... | collective-permute-start | bytes 860168 | tf_op jit(solution)/shard_map/ppermute | solution.py:67
  28.8 11.9 %collective-permute-done.2 = bf16[8,20,896]{2,1,0:T(8,128)(2,1)S(1)} collective-permute-done((bf16[8,20,896]{2,1,0:T(8,128)(2,1)S(1)}, bf16[8,20,896]{2,1,0:T(8,128)(2,1)S(1)}, u32[]{:S(2)}, u32[]{:S(2)}) %collective-permute-start.2) | collective-permute-done | bytes 286752 | tf_op jit(solution)/shard_map/ppermute | solution.py:67
  40.8 1.0 add_convert_fusion
  41.8 16.3 %all_to_all.25 = bf16[8,20,896]{2,1,0:T(8,128)(2,1)S(1)} all-to-all(bf16[8,20,896]{2,1,0:T(8,128)(2,1)} %add_convert_fusion), channel_id=1, replica_groups=mesh['dp'=2,'xh'=2,'y'=8,'z'=8,'c'=2] {'y'}, dimensions={0} | all-to-all | bytes 573440 | tf_op jit(solution)/shard_map/all_to_all | solution.py:52
  58.2 0.8 broadcast_in_dim.6
  59.0 7.1 %all-to-all-start.2 = ((bf16[8,20,896]{2,1,0:T(8,128)(2,1)}), bf16[8,20,896]{2,1,0:T(8,128)(2,1)S(1)}, u32[]{:S(2)}, u32[]{:S(2)}) async-start(bf16[8,20,896]{2,1,0:T(8,128)(2,1)} %broadcast_in_dim.6), calls=%async_computation.2 | async-start | bytes 688128 | tf_op jit(solution)/shard_map/all_to_all | solution.py:52
  66.1 0.1 fusion.17
  66.2 8.4 %all-to-all-done.2 = bf16[8,20,896]{2,1,0:T(8,128)(2,1)S(1)} async-done(((bf16[8,20,896]{2,1,0:T(8,128)(2,1)}), bf16[8,20,896]{2,1,0:T(8,128)(2,1)S(1)}, u32[]{:S(2)}, u32[]{:S(2)}) %all-to-all-start.2) | async-done | bytes 286752 | tf_op jit(solution)/shard_map/all_to_all | solution.py:52
  74.6 0.9 broadcast_in_dim.7
  75.5 6.8 %all-to-all-start.3 = ((bf16[16,20,896]{2,1,0:T(8,128)(2,1)}), bf16[16,20,896]{2,1,0:T(8,128)(2,1)S(1)}, u32[]{:S(2)}, u32[]{:S(2)}) async-start(bf16[16,20,896]{2,1,0:T(8,128)(2,1)} %broadcast_in_dim.7), calls=%async_computation.3 | async-start | bytes 1376256 | tf_op jit(solution)/shard_map/all_to_all | solution.py:52
  82.3 4.9 %collective-permute-start.3 = (bf16[8,20,896]{2,1,0:T(8,128)(2,1)S(1)}, bf16[8,20,896]{2,1,0:T(8,128)(2,1)S(1)}, u32[]{:S(2)}, u32[]{:S(2)}) collective-permute-start(bf16[8,20,896]{2,1,0:T(8,128)(2,1)S(1)} %all-to-all-done.2), channel_id=1, source_target_pairs={{0,128},{128,0},{1,129},{129,1},{2,130},{130,2},{3,131},{131,3},{4... | collective-permute-start | bytes 860168 | tf_op jit(solution)/shard_map/ppermute | solution.py:73
  87.2 10.8 %collective-permute-done.3 = bf16[8,20,896]{2,1,0:T(8,128)(2,1)S(1)} collective-permute-done((bf16[8,20,896]{2,1,0:T(8,128)(2,1)S(1)}, bf16[8,20,896]{2,1,0:T(8,128)(2,1)S(1)}, u32[]{:S(2)}, u32[]{:S(2)}) %collective-permute-start.3) | collective-permute-done | bytes 286752 | tf_op jit(solution)/shard_map/ppermute | solution.py:73
  98.1 0.1 fusion.3
  98.2 0.8 reshape.122
  99.0 0.8 reshape.124
  99.9 0.1 fusion.21
  100.0 0.1 reshape.121
  100.1 0.8 copy-done.3
  101.0 0.5 convolution_convert_fusion.3
  101.5 0.3 copy-done.9
  101.8 0.1 reshape.123
  101.9 0.8 copy-done.2
  102.8 0.5 convolution_convert_fusion.2
  103.3 0.1 broadcast_select_fusion.4
  103.5 0.1 copy-done.11
  103.6 0.2 reshape.125
  103.9 1.9 %collective-permute-start.4 = (bf16[16,10,1024]{2,1,0:T(8,128)(2,1)S(1)}, bf16[16,10,1024]{2,1,0:T(8,128)(2,1)S(1)}, u32[]{:S(2)}, u32[]{:S(2)}) collective-permute-start(bf16[16,10,1024]{2,1,0:T(8,128)(2,1)S(1)} %fusion.1), channel_id=1, source_target_pairs={{0,1},{1,0},{2,3},{3,2},{4,5},{5,4},{6,7},{7,6},{8,9},{9,8},{10,11... | collective-permute-start | bytes 983048 | tf_op jit(solution)/shard_map/ppermute | solution.py:85
  105.8 1.9 %collective-permute-done.4 = bf16[16,10,1024]{2,1,0:T(8,128)(2,1)S(1)} collective-permute-done((bf16[16,10,1024]{2,1,0:T(8,128)(2,1)S(1)}, bf16[16,10,1024]{2,1,0:T(8,128)(2,1)S(1)}, u32[]{:S(2)}, u32[]{:S(2)}) %collective-permute-start.4) | collective-permute-done | bytes 327712 | tf_op jit(solution)/shard_map/ppermute | solution.py:85
  107.7 1.1 fusion
  108.8 10.6 %all-to-all-start.4 = ((bf16[16,10,1024]{2,1,0:T(8,128)(2,1)}), bf16[16,10,1024]{2,1,0:T(8,128)(2,1)S(1)}, u32[]{:S(2)}, u32[]{:S(2)}) async-start(bf16[16,10,1024]{2,1,0:T(8,128)(2,1)} %fusion), calls=%async_computation.4 | async-start | bytes 1048576 | tf_op jit(solution)/shard_map/all_to_all | solution.py:52
  119.5 2.6 %convolution_convert_fusion = bf16[896,512]{1,0:T(8,128)(2,1)} fusion(bf16[320,896]{1,0:T(8,128)(2,1)S(1)} %copy-done.10, bf16[160,512]{1,0:T(8,128)(2,1)} %collective-permute-done.1, bf16[160,512]{1,0:T(8,128)(2,1)S(1)} %copy-done.5), kind=kOutput, calls=%fused_computation | convolution fusion | flops 294715392 | bytes 1818624 | tf_op jit(solution)/shard_map/dot_general | solution.py:16
  122.1 1.6 %convolution_convert_fusion.1 = bf16[512,896]{1,0:T(8,128)(2,1)} fusion(bf16[320,896]{1,0:T(8,128)(2,1)S(1)} %copy-done.12, bf16[160,512]{1,0:T(8,128)(2,1)S(1)} %copy-done.8, bf16[160,512]{1,0:T(8,128)(2,1)S(1)} %copy-done.6), kind=kOutput, calls=%fused_computation.1 | convolution fusion | flops 294715392 | bytes 1818624 | tf_op jit(solution)/shard_map/dot_general | solution.py:16
  123.7 11.5 %all-to-all-done.4 = bf16[16,10,1024]{2,1,0:T(8,128)(2,1)S(1)} async-done(((bf16[16,10,1024]{2,1,0:T(8,128)(2,1)}), bf16[16,10,1024]{2,1,0:T(8,128)(2,1)S(1)}, u32[]{:S(2)}, u32[]{:S(2)}) %all-to-all-start.4) | async-done | bytes 327712 | tf_op jit(solution)/shard_map/all_to_all | solution.py:52
  135.2 0.6 fusion.22
  (38 shorter events, 0.6 us)
Async XLA Ops:
  0.6 7.6 %copy-start = (bf16[896,512]{1,0:T(8,128)(2,1)S(1)}, bf16[896,512]{1,0:T(8,128)(2,1)}, u32[]{:S(2)}) copy-start(bf16[896,512]{1,0:T(8,128)(2,1)} %param.7) | copy-start | bytes 2752516
  0.6 7.6 %copy-start.4 = (bf16[160,512]{1,0:T(8,128)(2,1)S(1)}, bf16[160,512]{1,0:T(8,128)(2,1)}, u32[]{:S(2)}) copy-start(bf16[160,512]{1,0:T(8,128)(2,1)} %param.5) | copy-start | bytes 491524
  0.7 18.8 %collective-permute-start = (bf16[160,512]{1,0:T(8,128)(2,1)}, bf16[160,512]{1,0:T(8,128)(2,1)S(1)}, u32[]{:S(2)}, u32[]{:S(2)}) collective-permute-start(bf16[160,512]{1,0:T(8,128)(2,1)} %param.4), channel_id=1, source_target_pairs={{0,256},{256,0},{1,257},{257,1},{2,258},{258,2},{3,259},{259,3},{4... | collective-permute-start | bytes 491528 | tf_op jit(solution)/shard_map/ppermute | solution.py:62
  4.2 16.4 %collective-permute-start.1 = (bf16[160,512]{1,0:T(8,128)(2,1)}, bf16[160,512]{1,0:T(8,128)(2,1)}, u32[]{:S(2)}, u32[]{:S(2)}) collective-permute-start(bf16[160,512]{1,0:T(8,128)(2,1)} %param.5), channel_id=1, source_target_pairs={{0,256},{256,0},{1,257},{257,1},{2,258},{258,2},{3,259},{259,3},{4... | collective-permute-start | bytes 491528 | tf_op jit(solution)/shard_map/ppermute | solution.py:63
  10.0 10.2 %copy-start.1 = (bf16[512,896]{1,0:T(8,128)(2,1)S(1)}, bf16[512,896]{1,0:T(8,128)(2,1)}, u32[]{:S(2)}) copy-start(bf16[512,896]{1,0:T(8,128)(2,1)} %param.6) | copy-start | bytes 2752516
  10.0 31.8 %all-to-all-start = ((bf16[16,20,896]{2,1,0:T(8,128)(2,1)}), bf16[16,20,896]{2,1,0:T(8,128)(2,1)S(1)}, u32[]{:S(2)}, u32[]{:S(2)}) async-start(bf16[16,20,896]{2,1,0:T(8,128)(2,1)} %pad_maximum_fusion), calls=%async_computation | async-start | bytes 1376256 | tf_op jit(solution)/shard_map/all_to_all | solution.py:52
  19.5 0.7 copy-start.7
  24.0 16.8 %collective-permute-start.2 = (bf16[8,20,896]{2,1,0:T(8,128)(2,1)S(1)}, bf16[8,20,896]{2,1,0:T(8,128)(2,1)S(1)}, u32[]{:S(2)}, u32[]{:S(2)}) collective-permute-start(bf16[8,20,896]{2,1,0:T(8,128)(2,1)S(1)} %broadcast_select_fusion.2), channel_id=1, source_target_pairs={{0,128},{128,0},{1,129},{129,1},{2,130},{130,2},{3,131},{131,3},{4... | collective-permute-start | bytes 860168 | tf_op jit(solution)/shard_map/ppermute | solution.py:67
  59.0 15.6 %all-to-all-start.2 = ((bf16[8,20,896]{2,1,0:T(8,128)(2,1)}), bf16[8,20,896]{2,1,0:T(8,128)(2,1)S(1)}, u32[]{:S(2)}, u32[]{:S(2)}) async-start(bf16[8,20,896]{2,1,0:T(8,128)(2,1)} %broadcast_in_dim.6), calls=%async_computation.2 | async-start | bytes 688128 | tf_op jit(solution)/shard_map/all_to_all | solution.py:52
  75.5 24.4 %all-to-all-start.3 = ((bf16[16,20,896]{2,1,0:T(8,128)(2,1)}), bf16[16,20,896]{2,1,0:T(8,128)(2,1)S(1)}, u32[]{:S(2)}, u32[]{:S(2)}) async-start(bf16[16,20,896]{2,1,0:T(8,128)(2,1)} %broadcast_in_dim.7), calls=%async_computation.3 | async-start | bytes 1376256 | tf_op jit(solution)/shard_map/all_to_all | solution.py:52
  82.3 15.8 %collective-permute-start.3 = (bf16[8,20,896]{2,1,0:T(8,128)(2,1)S(1)}, bf16[8,20,896]{2,1,0:T(8,128)(2,1)S(1)}, u32[]{:S(2)}, u32[]{:S(2)}) collective-permute-start(bf16[8,20,896]{2,1,0:T(8,128)(2,1)S(1)} %all-to-all-done.2), channel_id=1, source_target_pairs={{0,128},{128,0},{1,129},{129,1},{2,130},{130,2},{3,131},{131,3},{4... | collective-permute-start | bytes 860168 | tf_op jit(solution)/shard_map/ppermute | solution.py:73
  100.0 1.0 copy-start.3
  101.0 0.8 copy-start.9
  101.8 1.0 copy-start.2
  102.8 0.8 copy-start.11
  103.9 3.8 %collective-permute-start.4 = (bf16[16,10,1024]{2,1,0:T(8,128)(2,1)S(1)}, bf16[16,10,1024]{2,1,0:T(8,128)(2,1)S(1)}, u32[]{:S(2)}, u32[]{:S(2)}) collective-permute-start(bf16[16,10,1024]{2,1,0:T(8,128)(2,1)S(1)} %fusion.1), channel_id=1, source_target_pairs={{0,1},{1,0},{2,3},{3,2},{4,5},{5,4},{6,7},{7,6},{8,9},{9,8},{10,11... | collective-permute-start | bytes 983048 | tf_op jit(solution)/shard_map/ppermute | solution.py:85
  108.8 10.6 %copy-start.5 = (bf16[160,512]{1,0:T(8,128)(2,1)S(1)}, bf16[160,512]{1,0:T(8,128)(2,1)}, u32[]{:S(2)}) copy-start(bf16[160,512]{1,0:T(8,128)(2,1)} %param.5) | copy-start | bytes 491524
  108.8 10.6 %copy-start.10 = (bf16[320,896]{1,0:T(8,128)(2,1)S(1)}, bf16[320,896]{1,0:T(8,128)(2,1)}, u32[]{:S(2)}) copy-start(bf16[320,896]{1,0:T(8,128)(2,1)} %copy-done.9) | copy-start | bytes 1720324
  108.8 26.3 %all-to-all-start.4 = ((bf16[16,10,1024]{2,1,0:T(8,128)(2,1)}), bf16[16,10,1024]{2,1,0:T(8,128)(2,1)S(1)}, u32[]{:S(2)}, u32[]{:S(2)}) async-start(bf16[16,10,1024]{2,1,0:T(8,128)(2,1)} %fusion), calls=%async_computation.4 | async-start | bytes 1048576 | tf_op jit(solution)/shard_map/all_to_all | solution.py:52
  119.4 2.6 %copy-start.6 = (bf16[160,512]{1,0:T(8,128)(2,1)S(1)}, bf16[160,512]{1,0:T(8,128)(2,1)}, u32[]{:S(2)}) copy-start(bf16[160,512]{1,0:T(8,128)(2,1)} %param.4) | copy-start | bytes 491524
  119.4 2.6 %copy-start.8 = (bf16[160,512]{1,0:T(8,128)(2,1)S(1)}, bf16[160,512]{1,0:T(8,128)(2,1)}, u32[]{:S(2)}) copy-start(bf16[160,512]{1,0:T(8,128)(2,1)} %copy-done.7) | copy-start | bytes 491524
  119.4 2.6 %copy-start.12 = (bf16[320,896]{1,0:T(8,128)(2,1)S(1)}, bf16[320,896]{1,0:T(8,128)(2,1)}, u32[]{:S(2)}) copy-start(bf16[320,896]{1,0:T(8,128)(2,1)} %copy-done.11) | copy-start | bytes 1720324

commit v3 on v1

v3 whole, which is shorter than its diff:
```python
import jax
import jax.numpy as jnp
from jax import lax
from jax.experimental import pallas as pl
from jax.experimental.pallas import tpu as pltpu
from jax.sharding import Mesh, PartitionSpec as P

ROW = ("xh", "y")
SWAP = [(0, 1), (1, 0)]
f32, bf16 = jnp.float32, jnp.bfloat16
SDS = jax.ShapeDtypeStruct


def dot(a, b, dims):
    return lax.dot_general(a, b, (dims, ((), ())), preferred_element_type=f32)


def call(kernel, outs, *args):
    spaces = [pltpu.SMEM if a.dtype == jnp.int32 else pltpu.VMEM for a in args]
    return pl.pallas_call(
        kernel,
        out_shape=outs,
        in_specs=[pl.BlockSpec(memory_space=s) for s in spaces],
        compiler_params=pltpu.CompilerParams(vmem_limit_bytes=24 * 2**20),
    )(*args)


def low(shape):
    return lax.broadcasted_iota(jnp.int32, shape, 0) < 4


def order_kernel(tokens_ref, cots_ref, out_ref):
    n = tokens_ref.shape[0]
    i = lax.broadcasted_iota(jnp.int32, (n, n), 0)
    t = lax.broadcasted_iota(jnp.int32, (n, n), 1)
    k = i - n * 4 // 5
    source = jnp.where(k < 0, 10 * (i >> 3) + (i & 7), 10 * (k >> 1) + 8 + (k & 1))
    pick = (source == t).astype(f32).astype(bf16)
    out_ref[:n] = dot(pick, tokens_ref[...], ((1,), (0,))).astype(bf16)
    out_ref[n:] = dot(pick, cots_ref[...], ((1,), (0,))).astype(bf16)


def partial_kernel(both_ref, up_ref, down_ref, out_ref):
    for d in range(2):
        base = 320 * d
        up = dot(both_ref[base : base + 160], up_ref[...], ((1,), (0,)))
        back = dot(both_ref[base + 160 : base + 320], down_ref[...], ((1,), (1,)))
        for k in range(8):
            out_ref[8 * d + k, 0:16] = up[16 * k : 16 * k + 16].astype(bf16)
            out_ref[8 * d + k, 16:32] = back[16 * k : 16 * k + 16].astype(bf16)
        for k in range(0, 8, 2):
            u, b = up[128 + 4 * k : 136 + 4 * k], back[128 + 4 * k : 136 + 4 * k]
            first = low(u.shape)
            out_ref[8 * d + k, 32:40] = jnp.where(first, u, pltpu.roll(b, 4, 0)).astype(bf16)
            out_ref[8 * d + k + 1, 32:40] = jnp.where(first, pltpu.roll(u, 4, 0), b).astype(bf16)


def gate(pre, back):
    sigma = 1.0 / (1.0 + jnp.exp(-pre))
    return pre * sigma, back * (sigma * (1.0 + pre * (1.0 - sigma)))


def activate_kernel(parts_ref, out_ref):
    terms = [parts_ref[i].astype(f32) for i in range(16)]
    while len(terms) > 1:
        terms = [a + b for a, b in zip(terms[::2], terms[1::2])]
    sums = terms[0].astype(bf16).astype(f32)
    hidden, grad = gate(sums[0:16], sums[16:32])
    tail = sums[32:40]
    tail_hidden, tail_grad = gate(tail, pltpu.roll(tail, 4, 0))
    tail = jnp.where(low(tail.shape), tail_hidden, pltpu.roll(tail_grad, 4, 0)).astype(bf16)
    hidden, grad = hidden.astype(bf16), grad.astype(bf16)
    for i in range(16):
        out_ref[i, 0:16] = hidden
        out_ref[i, 16:32] = grad
        out_ref[i, 32:40] = tail


def ends_kernel(core_ref, full_ref, up_ref, down_ref, hid_ref, grad_ref, keep_ref, send_ref):
    for d in range(2):
        base = 160 * d
        for k in range(8):
            hid_ref[base + 16 * k : base + 16 * k + 16] = full_ref[8 * d + k, 0:16]
            grad_ref[base + 16 * k : base + 16 * k + 16] = full_ref[8 * d + k, 16:32]
        for k in range(0, 8, 4):
            hids, grads = [], []
            for j in (0, 2):
                even = full_ref[8 * d + k + j, 32:40].astype(f32)
                odd = full_ref[8 * d + k + j + 1, 32:40].astype(f32)
                first = low(even.shape)
                hids.append(jnp.where(first, even, pltpu.roll(odd, 4, 0)))
                grads.append(jnp.where(first, pltpu.roll(even, 4, 0), odd))
            at = base + 128 + 4 * k
            hid_ref[at : at + 16] = jnp.concatenate(hids).astype(bf16)
            grad_ref[at : at + 16] = jnp.concatenate(grads).astype(bf16)
    near = core_ref[0] == 0
    pair = lax.broadcasted_iota(jnp.int32, (8, 128), 0) >> 1
    for d in range(2):
        rows = slice(160 * d, 160 * d + 160)
        out = dot(hid_ref[rows], down_ref[...], ((1,), (0,)))
        inp = dot(grad_ref[rows], up_ref[...], ((1,), (1,)))
        for k in range(8):
            r = 8 * d + k
            at = 128 + 8 * (k // 2)
            for part, full in enumerate((out, inp)):
                tails = [jnp.zeros((8, 128), f32)] * 2
                for l in range(4):
                    lanes = slice(128 * l, 128 * l + 128)
                    to = 32 * part + 8 * l
                    a, b = full[16 * k : 16 * k + 8, lanes], full[16 * k + 8 : 16 * k + 16, lanes]
                    keep_ref[r, to : to + 8] = jnp.where(near, a, b)
                    send_ref[r, to : to + 8] = jnp.where(near, b, a).astype(bf16)
                    tile = full[at : at + 8, lanes]
                    for c in range(2):
                        shift = (2 * l - 2 * c - 4 * (k % 2)) % 8
                        moved = pltpu.roll(tile, shift, 0) if shift else tile
                        tails[c] = jnp.where(pair == l, moved, tails[c])
                to = 64 + 8 * part
                keep_ref[r, to : to + 8] = jnp.where(near, tails[0], tails[1])
                send_ref[r, to : to + 8] = jnp.where(near, tails[1], tails[0]).astype(bf16)


def total_kernel(parts_ref, out_ref, inp_ref):
    terms = [parts_ref[i].astype(f32) for i in range(16)]
    while len(terms) > 1:
        terms = [a + b for a, b in zip(terms[::2], terms[1::2])]
    sums = terms[0]
    for part, ref in enumerate((out_ref, inp_ref)):
        tail = sums[64 + 8 * part : 72 + 8 * part]
        for l in range(4):
            to = 32 * part + 8 * l
            last = pltpu.roll(tail, 8 - 2 * l, 0) if l else tail
            rows = jnp.concatenate([sums[to : to + 8], last]).astype(bf16)
            ref[:, 128 * l : 128 * l + 128] = rows[:10]


def trade(parts, axis):
    return lax.all_to_all(parts, axis, 0, 0, tiled=True)


def body(tokens, cotangent, up_weight, down_weight):
    core = lax.axis_index("c")[None]
    count, width = tokens.shape
    hid = up_weight.shape[1]
    both = call(order_kernel, SDS((2 * count, width), bf16), tokens, cotangent)
    both, core = lax.optimization_barrier((lax.all_gather(both, "dp", axis=0, tiled=True), core))
    slabs = SDS((16, 40, hid), bf16)
    parts = trade(call(partial_kernel, slabs, both, up_weight, down_weight), ROW)
    full = trade(call(activate_kernel, slabs, parts), ROW)
    rows = SDS((2 * count, hid), bf16)
    hidden, grad_pre, keep, send = call(
        ends_kernel,
        (rows, rows, SDS((16, 80, 128), f32), SDS((16, 80, 128), bf16)),
        core,
        full,
        up_weight,
        down_weight,
    )
    ends = (keep + lax.ppermute(send, "c", SWAP).astype(f32)).astype(bf16)
    out_block = SDS((count // 16, width), bf16)
    output, input_grad = call(total_kernel, (out_block, out_block), trade(ends, ("dp", "z")))
    both = both.reshape(2, 2, count, width)
    acts, cots = both[:, 0].reshape(2 * count, width), both[:, 1].reshape(2 * count, width)
    up_grad = dot(acts, grad_pre, ((0,), (0,))).astype(bf16)
    down_grad = dot(hidden, cots, ((0,), (0,))).astype(bf16)
    return output, input_grad, up_grad, down_grad


def solution(mesh):
    fine = Mesh(mesh.devices.reshape(2, 2, 8, 8, 2), ("dp", "xh", "y", "z", "c"))
    split = ("dp", "z", "c")
    acts, up, down = P("dp", ROW), P(ROW, split), P(split, ROW)
    return jax.shard_map(
        body,
        mesh=fine,
        in_specs=(acts, acts, up, down),
        out_specs=(down, down, up, down),
        check_vma=False,
    )
```

time: 125 us -> 118 us (0.944)
  matrix products: 8.11 us -> 3.23 us
  blocking collectives: 86.7 us -> 82.5 us
  Pallas kernels: 0 us -> 3.32 us
  local copies, waits for them, and re-layouts: 5.81 us -> 3.14 us
  starting transfers between devices: 10.5 us -> 12.4 us
  waiting for transfers between devices: 8.41 us -> 9.96 us
  other arithmetic: 2.18 us -> 0.81 us
    dot_general x6 -> x2, matrix products: 8.11 us -> 3.23 us  [dot(): return lax.dot_general(a, b, (dims, ((), ())), preferred_element_type=f32)]
    all_to_all x3 -> x2, blocking collectives: 76.5 us -> 72.4 us  [trade(): return lax.all_to_all(parts, axis, 0, 0, tiled=True)]
    pallas_call x0 -> x5, Pallas kernels: none -> 3.32 us  [call(): pl.pallas_call(kernel, out_shape=outs, in_specs=[pl.BlockSpec(memory_spac...]
    unnamed x7 -> x10, local copies, waits for them, and re-layouts: 0.64 us -> 3.09 us
    another operation x2 -> x0, local copies, waits for them, and re-layouts: 2.16 us -> none  [body(): jnp.stack([out_part.reshape(16, 2, mini, width), in_part.reshape(16, 2, m...]
    ppermute x0 -> x1, starting transfers between devices: none -> 1.92 us  [body(): ends = (keep + lax.ppermute(send, 'c', SWAP).astype(f32)).astype(bf16)]
    ppermute x0 -> x1, waiting for transfers between devices: none -> 1.59 us  [body(): ends = (keep + lax.ppermute(send, 'c', SWAP).astype(f32)).astype(bf16)]
    reshape x4 -> x0, local copies, waits for them, and re-layouts: 1.28 us -> none  [the longest x1 0.93 us: body(): grad_pre = full[:, rows:].reshape(count, hid)]
  transfers between devices with their start and end apart: 1 -> 2, of which waited for: 1 -> 2; matrix products, arithmetic and copies ran while one was open for 3% -> 3% of each run, Pallas kernels for 0% -> 0%
where the time goes in v3:
time: 118 us; the launch traced here: 116 us
  blocking collectives  82.5 us (70%)
  starting transfers between devices  12.4 us (11%)
  waiting for transfers between devices  9.96 us (8%)
  Pallas kernels  3.32 us (3%)
  matrix products  3.23 us (3%)
  local copies, waits for them, and re-layouts  3.14 us (3%)
    all_to_all x2, blocking collectives, trade(): return lax.all_to_all(parts, axis, 0, 0, tiled=True)  72.4 us
    all_to_all x1, starting transfers between devices, trade(): return lax.all_to_all(parts, axis, 0, 0, tiled=True)  10.4 us
    all_gather x1, blocking collectives, body(): lax.all_gather(both, 'dp', axis=0, tiled=True)  10.1 us
    all_to_all x1, waiting for transfers between devices, trade(): return lax.all_to_all(parts, axis, 0, 0, tiled=True)  8.37 us
    pallas_call x5, Pallas kernels, call(): pl.pallas_call(kernel, out_shape=outs, in_specs=[pl.BlockSpec(memory_spac...  3.32 us
    dot_general x2, matrix products, dot(): return lax.dot_general(a, b, (dims, ((), ())), preferred_element_type=f32)  3.23 us
    unnamed x10, local copies, waits for them, and re-layouts  3.09 us
  transfers between devices with their start and end apart: 2, of which 2 were waited for; matrix products, arithmetic and copies ran while one was open for 3% of the time, Pallas kernels for 0%

profile of v3, /device:TPU:56, one launch (start us, length us, event | category | flops | bytes accessed | tf_op | source)
XLA Modules:
  0.0 116.1 jit_solution(1222097218144466536)
XLA Ops:
  0.6 0.0 copy-start
  0.6 0.0 copy-start.3
  0.7 1.0 copy-done.3
  1.6 0.0 copy-start.4
  1.6 0.9 copy-done.4
  2.6 0.2 shard_map.75
  2.8 10.1 %all_gather.3.both_ref = bf16[640,512]{1,0:T(8,128)(2,1)S(1)} all-gather(bf16[320,512]{1,0:T(8,128)(2,1)S(1)} %shard_map.75), channel_id=1, replica_groups=mesh['dp'=2,'xh'=2,'y'=8,'z'=8,'c'=2] {'dp'}, dimensions={0}, use_global_device_ids=true | all-gather | bytes 983040 | tf_op jit(solution)/shard_map/all_gather | solution.py:146
  12.9 0.0 copy-done
  12.9 0.0 copy-start.1
  12.9 1.2 %copy-done.1 = bf16[896,512]{1,0:T(8,128)(2,1)S(1)} copy-done((bf16[896,512]{1,0:T(8,128)(2,1)S(1)}, bf16[896,512]{1,0:T(8,128)(2,1)}, u32[]{:S(2)}) %copy-start.1) | copy-done | bytes 917528
  14.1 1.1 shard_map.76
  15.2 38.5 %all_to_all.15.parts_ref = bf16[16,40,896]{2,1,0:T(8,128)(2,1)S(1)} all-to-all(bf16[16,40,896]{2,1,0:T(8,128)(2,1)S(1)} %shard_map.76), channel_id=1, replica_groups=mesh['dp'=2,'xh'=2,'y'=8,'z'=8,'c'=2] {'xh','y'}, dimensions={0} | all-to-all | bytes 2293760 | tf_op jit(solution)/shard_map/all_to_all | solution.py:138
  53.7 0.2 shard_map.77
  53.9 0.0 copy-start.2
  53.9 33.9 %all_to_all.16.full_ref = bf16[16,40,896]{2,1,0:T(8,128)(2,1)S(1)} all-to-all(bf16[16,40,896]{2,1,0:T(8,128)(2,1)S(1)} %shard_map.77), channel_id=1, replica_groups=mesh['dp'=2,'xh'=2,'y'=8,'z'=8,'c'=2] {'xh','y'}, dimensions={0} | all-to-all | bytes 2293760 | tf_op jit(solution)/shard_map/all_to_all | solution.py:138
  87.8 0.0 copy-done.2
  87.8 1.1 shard_map.78
  89.0 1.9 %collective-permute-start = (bf16[16,80,128]{2,1,0:T(8,128)(2,1)S(1)}, bf16[16,80,128]{2,1,0:T(8,128)(2,1)S(1)}, u32[]{:S(2)}, u32[]{:S(2)}) collective-permute-start(bf16[16,80,128]{2,1,0:T(8,128)(2,1)S(1)} %get-tuple-element.15), channel_id=1, source_target_pairs={{0,1},{1,0},{2,3},{3,2},{4,5},{5,4},{6,7},{7,6},{8,9},{9,8},{10,11... | collective-permute-start | bytes 983048 | tf_op jit(solution)/shard_map/ppermute | solution.py:159
  90.9 1.6 %collective-permute-done = bf16[16,80,128]{2,1,0:T(8,128)(2,1)S(1)} collective-permute-done((bf16[16,80,128]{2,1,0:T(8,128)(2,1)S(1)}, bf16[16,80,128]{2,1,0:T(8,128)(2,1)S(1)}, u32[]{:S(2)}, u32[]{:S(2)}) %collective-permute-start) | collective-permute-done | bytes 327712 | tf_op jit(solution)/shard_map/ppermute | solution.py:159
  92.5 0.8 add_convert_fusion
  93.3 10.4 %all-to-all-start.2 = ((bf16[16,80,128]{2,1,0:T(8,128)(2,1)}), bf16[16,80,128]{2,1,0:T(8,128)(2,1)S(1)}, u32[]{:S(2)}, u32[]{:S(2)}) async-start(bf16[16,80,128]{2,1,0:T(8,128)(2,1)} %add_convert_fusion), calls=%async_computation.2 | async-start | bytes 655360 | tf_op jit(solution)/shard_map/all_to_all | solution.py:138
  103.8 0.1 fusion
  103.8 1.6 %convolution_convert_fusion.1 = bf16[512,896]{1,0:T(8,128)(2,1)} fusion(bf16[320,512]{1,0:T(8,128)(2,1)S(1)} %bitcast.9, bf16[320,896]{1,0:T(8,128)(2,1)S(1)} %get-tuple-element.18), kind=kOutput, calls=%fused_computation.1 | convolution fusion | flops 294060032 | bytes 1818624 | tf_op jit(solution)/shard_map/dot_general | solution.py:15
  105.5 1.6 %convolution_convert_fusion = bf16[896,512]{1,0:T(8,128)(2,1)} fusion(bf16[320,896]{1,0:T(8,128)(2,1)S(1)} %get-tuple-element.19, bf16[320,512]{1,0:T(8,128)(2,1)S(1)} %bitcast.10), kind=kOutput, calls=%fused_computation | convolution fusion | flops 294060032 | bytes 1818624 | tf_op jit(solution)/shard_map/dot_general | solution.py:15
  107.1 8.4 %all-to-all-done.2.parts_ref = bf16[16,80,128]{2,1,0:T(8,128)(2,1)S(1)} async-done(((bf16[16,80,128]{2,1,0:T(8,128)(2,1)}), bf16[16,80,128]{2,1,0:T(8,128)(2,1)S(1)}, u32[]{:S(2)}, u32[]{:S(2)}) %all-to-all-start.2) | async-done | bytes 327712 | tf_op jit(solution)/shard_map/all_to_all | solution.py:138
  115.4 0.7 shard_map.79
Async XLA Ops:
  0.6 12.3 %copy-start = (bf16[512,896]{1,0:T(8,128)(2,1)S(1)}, bf16[512,896]{1,0:T(8,128)(2,1)}, u32[]{:S(2)}) copy-start(bf16[512,896]{1,0:T(8,128)(2,1)} %up_ref.3) | copy-start | bytes 2752516
  0.6 1.0 copy-start.3
  1.6 0.9 copy-start.4
  12.9 1.2 %copy-start.1 = (bf16[896,512]{1,0:T(8,128)(2,1)S(1)}, bf16[896,512]{1,0:T(8,128)(2,1)}, u32[]{:S(2)}) copy-start(bf16[896,512]{1,0:T(8,128)(2,1)} %down_ref.3) | copy-start | bytes 2752516
  53.9 33.9 %copy-start.2 = (bf16[896,512]{1,0:T(8,128)(2,1)S(1)}, bf16[896,512]{1,0:T(8,128)(2,1)}, u32[]{:S(2)}) copy-start(bf16[896,512]{1,0:T(8,128)(2,1)} %down_ref.3) | copy-start | bytes 2752516
  89.0 3.5 %collective-permute-start = (bf16[16,80,128]{2,1,0:T(8,128)(2,1)S(1)}, bf16[16,80,128]{2,1,0:T(8,128)(2,1)S(1)}, u32[]{:S(2)}, u32[]{:S(2)}) collective-permute-start(bf16[16,80,128]{2,1,0:T(8,128)(2,1)S(1)} %get-tuple-element.15), channel_id=1, source_target_pairs={{0,1},{1,0},{2,3},{3,2},{4,5},{5,4},{6,7},{7,6},{8,9},{9,8},{10,11... | collective-permute-start | bytes 983048 | tf_op jit(solution)/shard_map/ppermute | solution.py:159
  93.3 22.1 %all-to-all-start.2 = ((bf16[16,80,128]{2,1,0:T(8,128)(2,1)}), bf16[16,80,128]{2,1,0:T(8,128)(2,1)S(1)}, u32[]{:S(2)}, u32[]{:S(2)}) async-start(bf16[16,80,128]{2,1,0:T(8,128)(2,1)} %add_convert_fusion), calls=%async_computation.2 | async-start | bytes 655360 | tf_op jit(solution)/shard_map/all_to_all | solution.py:138

commit v4 on v3

v4 whole, which is shorter than its diff:
```python
import jax
import jax.numpy as jnp
from jax import lax
from jax.experimental import pallas as pl
from jax.experimental.pallas import tpu as pltpu
from jax.sharding import Mesh, PartitionSpec as P

Y, PEERS, ROW = ("yh", "yl"), ("xh", "yh"), ("xh", "yh", "yl")
f32, bf16 = jnp.float32, jnp.bfloat16
SDS = jax.ShapeDtypeStruct


def dot(a, b, dims):
    return lax.dot_general(a, b, (dims, ((), ())), preferred_element_type=f32)


def call(kernel, outs, *args):
    spaces = [pltpu.SMEM if a.dtype == jnp.int32 else pltpu.VMEM for a in args]
    return pl.pallas_call(
        kernel,
        out_shape=outs,
        in_specs=[pl.BlockSpec(memory_space=s) for s in spaces],
        compiler_params=pltpu.CompilerParams(vmem_limit_bytes=24 * 2**20),
    )(*args)


def low(shape):
    return lax.broadcasted_iota(jnp.int32, shape, 0) < 4


def spots(d, j):
    return (24 * j, 16 * j) if d == 0 else (96 + 16 * j, 64 + 24 * j)


def place(refs, d, j, hid, grad, tail):
    h, g = spots(d, j)
    refs[0][h : h + 16] = hid.astype(refs[0].dtype)
    refs[1][g : g + 16] = grad.astype(refs[1].dtype)
    at = (h, g)[d] + 16
    refs[d][at : at + 8] = tail.astype(refs[d].dtype)


def take(refs, d, j):
    h, g = spots(d, j)
    at = (h, g)[d] + 16
    hid, grad, tail = refs[0][h : h + 16], refs[1][g : g + 16], refs[d][at : at + 8]
    return hid.astype(f32), grad.astype(f32), tail.astype(f32)


def order_rows(rows):
    n = rows.shape[0]
    i = lax.broadcasted_iota(jnp.int32, (n, n), 0)
    t = lax.broadcasted_iota(jnp.int32, (n, n), 1)
    k = i - n * 4 // 5
    source = jnp.where(k < 0, 10 * (i >> 3) + (i & 7), 10 * (k >> 1) + 8 + (k & 1))
    return dot((source == t).astype(f32).astype(bf16), rows, ((1,), (0,))).astype(bf16)


def partial_kernel(side_ref, both_ref, up_ref, down_ref, acts_ref, cots_ref, keep_h, keep_g, send_h, send_g):
    even = side_ref[0] == 0
    for d in range(2):
        at, rows = 320 * d, slice(160 * d, 160 * d + 160)
        acts_ref[rows] = order_rows(both_ref[at : at + 160])
        cots_ref[rows] = order_rows(both_ref[at + 160 : at + 320])
        up = dot(acts_ref[rows], up_ref[...], ((1,), (0,)))
        back = dot(cots_ref[rows], down_ref[...], ((1,), (1,)))
        for j in range(4):
            m, n = slice(32 * j, 32 * j + 16), slice(32 * j + 16, 32 * j + 32)
            u, b = up[128 + 8 * j : 136 + 8 * j], back[128 + 8 * j : 136 + 8 * j]
            first = low(u.shape)
            near = up[m], back[m], jnp.where(first, u, pltpu.roll(b, 4, 0))
            far = up[n], back[n], jnp.where(first, pltpu.roll(u, 4, 0), b)
            place((keep_h, keep_g), d, j, *(jnp.where(even, x, y) for x, y in zip(near, far)))
            place((send_h, send_g), d, j, *(jnp.where(even, y, x) for x, y in zip(near, far)))


def merge_kernel(keep_h, keep_g, recv_h, recv_g, out_ref):
    for d in range(2):
        for j in range(4):
            own, got = take((keep_h, keep_g), d, j), take((recv_h, recv_g), d, j)
            hid, grad, tail = ((a + b).astype(bf16) for a, b in zip(own, got))
            out_ref[4 * d + j, 0:16] = hid
            out_ref[4 * d + j, 16:32] = grad
            out_ref[4 * d + j, 32:40] = tail


def split_kernel(full_ref, send_h, send_g):
    for d in range(2):
        for j in range(4):
            slab = full_ref.at[4 * d + j]
            place((send_h, send_g), d, j, slab[0:16], slab[16:32], slab[32:40])


def gate(pre, back):
    sigma = 1.0 / (1.0 + jnp.exp(-pre))
    return pre * sigma, back * (sigma * (1.0 + pre * (1.0 - sigma)))


def activate_kernel(parts_ref, out_ref):
    terms = [parts_ref[i].astype(f32) for i in range(8)]
    while len(terms) > 1:
        terms = [a + b for a, b in zip(terms[::2], terms[1::2])]
    sums = terms[0].astype(bf16).astype(f32)
    hidden, grad = gate(sums[0:16], sums[16:32])
    tail = sums[32:40]
    tail_hidden, tail_grad = gate(tail, pltpu.roll(tail, 4, 0))
    tail = jnp.where(low(tail.shape), tail_hidden, pltpu.roll(tail_grad, 4, 0)).astype(bf16)
    hidden, grad = hidden.astype(bf16), grad.astype(bf16)
    for i in range(8):
        out_ref[i, 0:16] = hidden
        out_ref[i, 16:32] = grad
        out_ref[i, 32:40] = tail


def ends_kernel(core_ref, side_ref, full_ref, recv_h, recv_g, up_ref, down_ref, hid_ref, grad_ref, keep_ref, send_ref):
    is_even = side_ref[0] == 0
    for d in range(2):
        base = 160 * d
        hids, grads = [], []
        for j in range(4):
            slab = full_ref.at[4 * d + j]
            own = [slab[0:16].astype(f32), slab[16:32].astype(f32), slab[32:40].astype(f32)]
            got = take((recv_h, recv_g), d, j)
            for k, (one, two) in enumerate(((own, got), (got, own))):
                at = base + 32 * j + 16 * k
                hid_ref[at : at + 16] = jnp.where(is_even, one[0], two[0]).astype(bf16)
                grad_ref[at : at + 16] = jnp.where(is_even, one[1], two[1]).astype(bf16)
            even, odd = jnp.where(is_even, own[2], got[2]), jnp.where(is_even, got[2], own[2])
            first = low(even.shape)
            hids.append(jnp.where(first, even, pltpu.roll(odd, 4, 0)))
            grads.append(jnp.where(first, pltpu.roll(even, 4, 0), odd))
        hid_ref[base + 128 : base + 160] = jnp.concatenate(hids).astype(bf16)
        grad_ref[base + 128 : base + 160] = jnp.concatenate(grads).astype(bf16)
    near = core_ref[0] == 0
    pair = lax.broadcasted_iota(jnp.int32, (8, 128), 0) >> 1
    for d in range(2):
        rows = slice(160 * d, 160 * d + 160)
        out = dot(hid_ref[rows], down_ref[...], ((1,), (0,)))
        inp = dot(grad_ref[rows], up_ref[...], ((1,), (1,)))
        for k in range(8):
            r = 8 * d + k
            at = 128 + 8 * (k // 2)
            for part, full in enumerate((out, inp)):
                tails = [jnp.zeros((8, 128), f32)] * 2
                for l in range(4):
                    lanes = slice(128 * l, 128 * l + 128)
                    to = 32 * part + 8 * l
                    a, b = full[16 * k : 16 * k + 8, lanes], full[16 * k + 8 : 16 * k + 16, lanes]
                    keep_ref[r, to : to + 8] = jnp.where(near, a, b)
                    send_ref[r, to : to + 8] = jnp.where(near, b, a).astype(bf16)
                    tile = full[at : at + 8, lanes]
                    for c in range(2):
                        shift = (2 * l - 2 * c - 4 * (k % 2)) % 8
                        moved = pltpu.roll(tile, shift, 0) if shift else tile
                        tails[c] = jnp.where(pair == l, moved, tails[c])
                to = 64 + 8 * part
                keep_ref[r, to : to + 8] = jnp.where(near, tails[0], tails[1])
                send_ref[r, to : to + 8] = jnp.where(near, tails[1], tails[0]).astype(bf16)


def total_kernel(parts_ref, out_ref, inp_ref):
    terms = [parts_ref[i].astype(f32) for i in range(16)]
    while len(terms) > 1:
        terms = [a + b for a, b in zip(terms[::2], terms[1::2])]
    sums = terms[0]
    for part, ref in enumerate((out_ref, inp_ref)):
        tail = sums[64 + 8 * part : 72 + 8 * part]
        for l in range(4):
            to = 32 * part + 8 * l
            last = pltpu.roll(tail, 8 - 2 * l, 0) if l else tail
            rows = jnp.concatenate([sums[to : to + 8], last]).astype(bf16)
            ref[:, 128 * l : 128 * l + 128] = rows[:10]


def trade(parts, axis):
    return lax.all_to_all(parts, axis, 0, 0, tiled=True)


def core_kernel(core_ref, keep_ref, cores_ref, out_ref):
    out_ref[...] = (keep_ref[...] + cores_ref[1 - core_ref[0]].astype(f32)).astype(bf16)


def neighbours(to_up, to_down):
    up = lax.ppermute(to_up, Y, [(i, (i + 1) % 8) for i in range(8)])
    return up, lax.ppermute(to_down, Y, [(i, (i - 1) % 8) for i in range(8)])


def body(tokens, cotangent, up_weight, down_weight):
    core, side = lax.axis_index("c")[None], lax.axis_index("yl")[None]
    count, width = tokens.shape
    hid = up_weight.shape[1]
    both = lax.all_gather(jnp.concatenate([tokens, cotangent]), "dp", axis=0, tiled=True)
    both, core, side = lax.optimization_barrier((both, core, side))
    wide, note = SDS((160, hid), f32), SDS((160, hid), bf16)
    ordered = SDS((2 * count, width), bf16)
    outs = (ordered, ordered, wide, wide, note, note)
    acts, cots, *keep, to_up, to_down = call(partial_kernel, outs, side, both, up_weight, down_weight)
    slabs = SDS((8, 40, hid), bf16)
    parts = trade(call(merge_kernel, slabs, *keep, *neighbours(to_up, to_down)), PEERS)
    full = trade(call(activate_kernel, slabs, parts), PEERS)
    others = neighbours(*call(split_kernel, (note, note), full))
    rows = SDS((2 * count, hid), bf16)
    hidden, grad_pre, keep, send = call(
        ends_kernel,
        (rows, rows, SDS((16, 80, 128), f32), SDS((16, 80, 128), bf16)),
        core,
        side,
        full,
        *others,
        up_weight,
        down_weight,
    )
    cores = lax.all_gather(send, "c", axis=0)
    ends = trade(call(core_kernel, SDS(send.shape, bf16), core, keep, cores), ("dp", "z"))
    out_block = SDS((count // 16, width), bf16)
    output, input_grad = call(total_kernel, (out_block, out_block), ends)
    up_grad = dot(acts, grad_pre, ((0,), (0,))).astype(bf16)
    down_grad = dot(hidden, cots, ((0,), (0,))).astype(bf16)
    return output, input_grad, up_grad, down_grad


def solution(mesh):
    fine = Mesh(mesh.devices.reshape(2, 2, 4, 2, 8, 2), ("dp", "xh", "yh", "yl", "z", "c"))
    split = ("dp", "z", "c")
    acts, up, down = P("dp", ROW), P(ROW, split), P(split, ROW)
    return jax.shard_map(
        body,
        mesh=fine,
        in_specs=(acts, acts, up, down),
        out_specs=(down, down, up, down),
        check_vma=False,
    )
```

time: 118 us -> 115 us (0.975)
  the two profiles are of different devices: /device:TPU:56 before, /device:TPU:8 now
where the time goes in v4:
time: 115 us; the launch traced here: 114 us
  blocking collectives  59.7 us (52%)
  starting transfers between devices  23.6 us (21%)
  waiting for transfers between devices  20.4 us (18%)
  Pallas kernels  4.24 us (4%)
  matrix products  3.23 us (3%)
  local copies, waits for them, and re-layouts  1.19 us (1%)
    all_to_all x2, blocking collectives, trade(): return lax.all_to_all(parts, axis, 0, 0, tiled=True)  47.3 us
    all_to_all x1, starting transfers between devices, trade(): return lax.all_to_all(parts, axis, 0, 0, tiled=True)  10.5 us
    all_gather x1, blocking collectives, body(): lax.all_gather(jnp.concatenate([tokens, cotangent]), 'dp', axis=0, tiled=...  10.1 us
    all_to_all x1, waiting for transfers between devices, trade(): return lax.all_to_all(parts, axis, 0, 0, tiled=True)  8.43 us
    ppermute x2, starting transfers between devices, neighbours(): up = lax.ppermute(to_up, Y, [(i, (i + 1) % 8) for i in range(8)])  7.27 us
    ppermute x2, waiting for transfers between devices, neighbours(): return (up, lax.ppermute(to_down, Y, [(i, (i - 1) % 8) for i in range(8)]))  6.65 us
    ppermute x2, starting transfers between devices, neighbours(): return (up, lax.ppermute(to_down, Y, [(i, (i - 1) % 8) for i in range(8)]))  5.84 us
    ppermute x2, waiting for transfers between devices, neighbours(): up = lax.ppermute(to_up, Y, [(i, (i + 1) % 8) for i in range(8)])  5.34 us
  transfers between devices with their start and end apart: 5, of which 5 were waited for; matrix products, arithmetic and copies ran while one was open for 3% of the time, Pallas kernels for 0%

profile of v4, /device:TPU:8, one launch (start us, length us, event | category | flops | bytes accessed | tf_op | source)
XLA Modules:
  0.0 114.2 jit_solution(12422086297155484515)
XLA Ops:
  0.6 0.0 copy-start
  0.6 1.1 pad_maximum_fusion
  1.7 10.1 %all_gather.9.both_ref = bf16[640,512]{1,0:T(8,128)(2,1)S(1)} all-gather(bf16[320,512]{1,0:T(8,128)(2,1)S(1)} %pad_maximum_fusion), channel_id=1, replica_groups=mesh['dp'=2,'xh'=2,'yh'=4,'yl'=2,'z'=8,'c'=2] {'dp'}, dimensions={0}, use_global_device_ids=true | all-gather | bytes 983040 | tf_op jit(solution)/shard_map/all_gather | solution.py:192
  11.9 0.0 copy-done
  11.9 0.0 copy-start.1
  11.9 1.2 %copy-done.1 = bf16[896,512]{1,0:T(8,128)(2,1)S(1)} copy-done((bf16[896,512]{1,0:T(8,128)(2,1)S(1)}, bf16[896,512]{1,0:T(8,128)(2,1)}, u32[]{:S(2)}) %copy-start.1) | copy-done | bytes 917528
  13.1 1.3 %shard_map.75 = (bf16[320,512]{1,0:T(8,128)(2,1)S(1)}, bf16[320,512]{1,0:T(8,128)(2,1)S(1)}, f32[160,896]{1,0:T(8,128)S(1)}, f32[160,896]{1,0:T(8,128)S(1)}, bf1...) custom-call(s32[1]{0:T(128)} %bitcast.1.side_ref, bf16[640,512]{1,0:T(8,128)(2,1)S(1)} %all_gather.9.both_ref, ...), custom_call_target="tpu_custom_call" | custom-call | tf_op jit(solution)/shard_map/pallas_call | solution.py:19
  14.4 3.5 %collective-permute-start = (bf16[160,896]{1,0:T(8,128)(2,1)S(1)}, bf16[160,896]{1,0:T(8,128)(2,1)S(1)}, u32[]{:S(2)}, u32[]{:S(2)}) collective-permute-start(bf16[160,896]{1,0:T(8,128)(2,1)S(1)} %get-tuple-element.26), channel_id=1, source_target_pairs={{0,16},{16,32},{32,48},{48,64},{64,80},{80,96},{96,112},{112,0},{1... | collective-permute-start | bytes 860168 | tf_op jit(solution)/shard_map/ppermute | solution.py:184
  17.9 3.8 %collective-permute-start.1 = (bf16[160,896]{1,0:T(8,128)(2,1)S(1)}, bf16[160,896]{1,0:T(8,128)(2,1)S(1)}, u32[]{:S(2)}, u32[]{:S(2)}) collective-permute-start(bf16[160,896]{1,0:T(8,128)(2,1)S(1)} %get-tuple-element.27), channel_id=1, source_target_pairs={{0,112},{16,0},{32,16},{48,32},{64,48},{80,64},{96,80},{112,96},{1... | collective-permute-start | bytes 860168 | tf_op jit(solution)/shard_map/ppermute | solution.py:185
  21.7 2.7 %collective-permute-done.recv_h = bf16[160,896]{1,0:T(8,128)(2,1)S(1)} collective-permute-done((bf16[160,896]{1,0:T(8,128)(2,1)S(1)}, bf16[160,896]{1,0:T(8,128)(2,1)S(1)}, u32[]{:S(2)}, u32[]{:S(2)}) %collective-permute-start) | collective-permute-done | bytes 286752 | tf_op jit(solution)/shard_map/ppermute | solution.py:184
  24.4 2.9 %collective-permute-done.1.recv_g = bf16[160,896]{1,0:T(8,128)(2,1)S(1)} collective-permute-done((bf16[160,896]{1,0:T(8,128)(2,1)S(1)}, bf16[160,896]{1,0:T(8,128)(2,1)S(1)}, u32[]{:S(2)}, u32[]{:S(2)}) %collective-permute-start.1) | collective-permute-done | bytes 286752 | tf_op jit(solution)/shard_map/ppermute | solution.py:185
  27.2 0.1 shard_map.76
  27.3 26.4 %all_to_all.15.parts_ref = bf16[8,40,896]{2,1,0:T(8,128)(2,1)S(1)} all-to-all(bf16[8,40,896]{2,1,0:T(8,128)(2,1)S(1)} %shard_map.76), channel_id=1, replica_groups=mesh['dp'=2,'xh'=2,'yh'=4,'yl'=2,'z'=8,'c'=2] {'xh','yh'}, dimensions={0} | all-to-all | bytes 1146880 | tf_op jit(solution)/shard_map/all_to_all | solution.py:176
  53.7 0.1 shard_map.77
  53.9 0.0 copy-start.2
  53.9 20.9 %all_to_all.16.full_ref = bf16[8,40,896]{2,1,0:T(8,128)(2,1)S(1)} all-to-all(bf16[8,40,896]{2,1,0:T(8,128)(2,1)S(1)} %shard_map.77), channel_id=1, replica_groups=mesh['dp'=2,'xh'=2,'yh'=4,'yl'=2,'z'=8,'c'=2] {'xh','yh'}, dimensions={0} | all-to-all | bytes 1146880 | tf_op jit(solution)/shard_map/all_to_all | solution.py:176
  74.9 3.8 %collective-permute-start.2 = (bf16[160,896]{1,0:T(8,128)(2,1)S(1)}, bf16[160,896]{1,0:T(8,128)(2,1)S(1)}, u32[]{:S(2)}, u32[]{:S(2)}) collective-permute-start(bf16[160,896]{1,0:T(8,128)(2,1)S(1)} %get-tuple-element.28), channel_id=1, source_target_pairs={{0,16},{16,32},{32,48},{48,64},{64,80},{80,96},{96,112},{112,0},{1... | collective-permute-start | bytes 860168 | tf_op jit(solution)/shard_map/ppermute | solution.py:184
  78.7 2.1 %collective-permute-start.3 = (bf16[160,896]{1,0:T(8,128)(2,1)S(1)}, bf16[160,896]{1,0:T(8,128)(2,1)S(1)}, u32[]{:S(2)}, u32[]{:S(2)}) collective-permute-start(bf16[160,896]{1,0:T(8,128)(2,1)S(1)} %get-tuple-element.29), channel_id=1, source_target_pairs={{0,112},{16,0},{32,16},{48,32},{64,48},{80,64},{96,80},{112,96},{1... | collective-permute-start | bytes 860168 | tf_op jit(solution)/shard_map/ppermute | solution.py:185
  80.7 2.7 %collective-permute-done.2.recv_h = bf16[160,896]{1,0:T(8,128)(2,1)S(1)} collective-permute-done((bf16[160,896]{1,0:T(8,128)(2,1)S(1)}, bf16[160,896]{1,0:T(8,128)(2,1)S(1)}, u32[]{:S(2)}, u32[]{:S(2)}) %collective-permute-start.2) | collective-permute-done | bytes 286752 | tf_op jit(solution)/shard_map/ppermute | solution.py:184
  83.4 3.8 %collective-permute-done.3.recv_g = bf16[160,896]{1,0:T(8,128)(2,1)S(1)} collective-permute-done((bf16[160,896]{1,0:T(8,128)(2,1)S(1)}, bf16[160,896]{1,0:T(8,128)(2,1)S(1)}, u32[]{:S(2)}, u32[]{:S(2)}) %collective-permute-start.3) | collective-permute-done | bytes 286752 | tf_op jit(solution)/shard_map/ppermute | solution.py:185
  87.2 0.0 copy-done.2
  87.2 1.2 %shard_map.79 = (bf16[320,896]{1,0:T(8,128)(2,1)S(1)}, bf16[320,896]{1,0:T(8,128)(2,1)S(1)}, f32[16,80,128]{2,1,0:T(8,128)S(1)}, bf16[16,80,128]{2,1,0:T(8,128)(2,1)S(1)}) custom-call(s32[1]{0:T(128)} %bitcast.core_ref, s32[1]{0:T(128)} %bitcast.1.side_ref, bf16[8,40,896]{2,1,0:T(8,128)(2,1)S(1)} %all_to_all.16.full_ref, ...), custom_call_target="tpu_custom_call" | custom-call | tf_op jit(solution)/shard_map/pallas_call | solution.py:19
  88.4 2.3 %all-gather = bf16[32,80,128]{2,1,0:T(8,128)(2,1)S(1)} all-gather(bf16[16,80,128]{2,1,0:T(8,128)(2,1)S(1)} %get-tuple-element.31), channel_id=2, replica_groups=mesh['dp'=2,'xh'=2,'yh'=4,'yl'=2,'z'=8,'c'=2] {'c'}, dimensions={0}, use_global_device_ids=true | all-gather | bytes 983040 | tf_op jit(solution)/shard_map/all_gather | solution.py:213
  90.7 0.8 shard_map.80
  91.4 10.5 %all-to-all-start.2 = ((bf16[16,80,128]{2,1,0:T(8,128)(2,1)}), bf16[16,80,128]{2,1,0:T(8,128)(2,1)S(1)}, u32[]{:S(2)}, u32[]{:S(2)}) async-start(bf16[16,80,128]{2,1,0:T(8,128)(2,1)} %shard_map.80), calls=%async_computation.2 | async-start | bytes 655360 | tf_op jit(solution)/shard_map/all_to_all | solution.py:176
  101.9 1.6 %convolution_convert_fusion.1 = bf16[512,896]{1,0:T(8,128)(2,1)} fusion(bf16[320,512]{1,0:T(8,128)(2,1)S(1)} %get-tuple-element.34, bf16[320,896]{1,0:T(8,128)(2,1)S(1)} %get-tuple-element.35), kind=kOutput, calls=%fused_computation.1 | convolution fusion | flops 294060032 | bytes 1818624 | tf_op jit(solution)/shard_map/dot_general | solution.py:14
  103.6 1.6 %convolution_convert_fusion = bf16[896,512]{1,0:T(8,128)(2,1)} fusion(bf16[320,896]{1,0:T(8,128)(2,1)S(1)} %get-tuple-element.36, bf16[320,512]{1,0:T(8,128)(2,1)S(1)} %get-tuple-element.37), kind=kOutput, calls=%fused_computation | convolution fusion | flops 294060032 | bytes 1818624 | tf_op jit(solution)/shard_map/dot_general | solution.py:14
  105.2 8.4 %all-to-all-done.2.parts_ref = bf16[16,80,128]{2,1,0:T(8,128)(2,1)S(1)} async-done(((bf16[16,80,128]{2,1,0:T(8,128)(2,1)}), bf16[16,80,128]{2,1,0:T(8,128)(2,1)S(1)}, u32[]{:S(2)}, u32[]{:S(2)}) %all-to-all-start.2) | async-done | bytes 327712 | tf_op jit(solution)/shard_map/all_to_all | solution.py:176
  113.6 0.7 shard_map.81
  (1 shorter events, 0.0 us)
Async XLA Ops:
  0.6 11.2 %copy-start = (bf16[512,896]{1,0:T(8,128)(2,1)S(1)}, bf16[512,896]{1,0:T(8,128)(2,1)}, u32[]{:S(2)}) copy-start(bf16[512,896]{1,0:T(8,128)(2,1)} %up_ref.3) | copy-start | bytes 2752516
  11.9 1.2 %copy-start.1 = (bf16[896,512]{1,0:T(8,128)(2,1)S(1)}, bf16[896,512]{1,0:T(8,128)(2,1)}, u32[]{:S(2)}) copy-start(bf16[896,512]{1,0:T(8,128)(2,1)} %down_ref.3) | copy-start | bytes 2752516
  14.4 10.0 %collective-permute-start = (bf16[160,896]{1,0:T(8,128)(2,1)S(1)}, bf16[160,896]{1,0:T(8,128)(2,1)S(1)}, u32[]{:S(2)}, u32[]{:S(2)}) collective-permute-start(bf16[160,896]{1,0:T(8,128)(2,1)S(1)} %get-tuple-element.26), channel_id=1, source_target_pairs={{0,16},{16,32},{32,48},{48,64},{64,80},{80,96},{96,112},{112,0},{1... | collective-permute-start | bytes 860168 | tf_op jit(solution)/shard_map/ppermute | solution.py:184
  17.9 9.3 %collective-permute-start.1 = (bf16[160,896]{1,0:T(8,128)(2,1)S(1)}, bf16[160,896]{1,0:T(8,128)(2,1)S(1)}, u32[]{:S(2)}, u32[]{:S(2)}) collective-permute-start(bf16[160,896]{1,0:T(8,128)(2,1)S(1)} %get-tuple-element.27), channel_id=1, source_target_pairs={{0,112},{16,0},{32,16},{48,32},{64,48},{80,64},{96,80},{112,96},{1... | collective-permute-start | bytes 860168 | tf_op jit(solution)/shard_map/ppermute | solution.py:185
  53.9 33.3 %copy-start.2 = (bf16[896,512]{1,0:T(8,128)(2,1)S(1)}, bf16[896,512]{1,0:T(8,128)(2,1)}, u32[]{:S(2)}) copy-start(bf16[896,512]{1,0:T(8,128)(2,1)} %down_ref.3) | copy-start | bytes 2752516
  74.9 8.5 %collective-permute-start.2 = (bf16[160,896]{1,0:T(8,128)(2,1)S(1)}, bf16[160,896]{1,0:T(8,128)(2,1)S(1)}, u32[]{:S(2)}, u32[]{:S(2)}) collective-permute-start(bf16[160,896]{1,0:T(8,128)(2,1)S(1)} %get-tuple-element.28), channel_id=1, source_target_pairs={{0,16},{16,32},{32,48},{48,64},{64,80},{80,96},{96,112},{112,0},{1... | collective-permute-start | bytes 860168 | tf_op jit(solution)/shard_map/ppermute | solution.py:184
  78.7 8.5 %collective-permute-start.3 = (bf16[160,896]{1,0:T(8,128)(2,1)S(1)}, bf16[160,896]{1,0:T(8,128)(2,1)S(1)}, u32[]{:S(2)}, u32[]{:S(2)}) collective-permute-start(bf16[160,896]{1,0:T(8,128)(2,1)S(1)} %get-tuple-element.29), channel_id=1, source_target_pairs={{0,112},{16,0},{32,16},{48,32},{64,48},{80,64},{96,80},{112,96},{1... | collective-permute-start | bytes 860168 | tf_op jit(solution)/shard_map/ppermute | solution.py:185
  91.4 22.1 %all-to-all-start.2 = ((bf16[16,80,128]{2,1,0:T(8,128)(2,1)}), bf16[16,80,128]{2,1,0:T(8,128)(2,1)S(1)}, u32[]{:S(2)}, u32[]{:S(2)}) async-start(bf16[16,80,128]{2,1,0:T(8,128)(2,1)} %shard_map.80), calls=%async_computation.2 | async-start | bytes 655360 | tf_op jit(solution)/shard_map/all_to_all | solution.py:176

commit v5 on v4

--- a/solution.py
+++ b/solution.py
@@ -15,11 +15,10 @@
 
 
 def call(kernel, outs, *args):
-    spaces = [pltpu.SMEM if a.dtype == jnp.int32 else pltpu.VMEM for a in args]
     return pl.pallas_call(
         kernel,
         out_shape=outs,
-        in_specs=[pl.BlockSpec(memory_space=s) for s in spaces],
+        in_specs=[pl.BlockSpec(memory_space=pltpu.SMEM) if a.dtype == jnp.int32 else pl.BlockSpec() for a in args],
         compiler_params=pltpu.CompilerParams(vmem_limit_bytes=24 * 2**20),
     )(*args)
 
@@ -29,7 +28,11 @@
 
 
 def spots(d, j):
-    return (24 * j, 16 * j) if d == 0 else (96 + 16 * j, 64 + 24 * j)
+    return (24 * j, 16 * j) if d == 0 else (16 * j, 24 * j)
+
+
+def halves(refs, d):
+    return (refs[0].at[0:96], refs[1].at[0:64]) if d == 0 else (refs[0].at[96:160], refs[1].at[64:160])
 
 
 def place(refs, d, j, hid, grad, tail):
@@ -45,6 +48,10 @@
     at = (h, g)[d] + 16
     hid, grad, tail = refs[0][h : h + 16], refs[1][g : g + 16], refs[d][at : at + 8]
     return hid.astype(f32), grad.astype(f32), tail.astype(f32)
+
+
+def group(dp_ref, i):
+    return dp_ref[0] if i == 0 else 1 - dp_ref[0]
 
 
 def order_rows(rows):
@@ -56,39 +63,36 @@
     return dot((source == t).astype(f32).astype(bf16), rows, ((1,), (0,))).astype(bf16)
 
 
-def partial_kernel(side_ref, both_ref, up_ref, down_ref, acts_ref, cots_ref, keep_h, keep_g, send_h, send_g):
+def partial_kernel(side_ref, both_ref, up_ref, down_ref, acts_ref, cots_ref, keep_ref, send_ref):
     even = side_ref[0] == 0
-    for d in range(2):
-        at, rows = 320 * d, slice(160 * d, 160 * d + 160)
-        acts_ref[rows] = order_rows(both_ref[at : at + 160])
-        cots_ref[rows] = order_rows(both_ref[at + 160 : at + 320])
-        up = dot(acts_ref[rows], up_ref[...], ((1,), (0,)))
-        back = dot(cots_ref[rows], down_ref[...], ((1,), (1,)))
+    acts_ref[...] = order_rows(both_ref[0:160])
+    cots_ref[...] = order_rows(both_ref[160:320])
+    up = dot(acts_ref[...], up_ref[...], ((1,), (0,)))
+    back = dot(cots_ref[...], down_ref[...], ((1,), (1,)))
+    for j in range(4):
+        m, n = slice(32 * j, 32 * j + 16), slice(32 * j + 16, 32 * j + 32)
+        u, b = up[128 + 8 * j : 136 + 8 * j], back[128 + 8 * j : 136 + 8 * j]
+        first = low(u.shape)
+        near = up[m], back[m], jnp.where(first, u, pltpu.roll(b, 4, 0))
+        far = up[n], back[n], jnp.where(first, pltpu.roll(u, 4, 0), b)
+        for x, y, at, size in zip(near, far, (0, 16, 32), (16, 16, 8)):
+            at = slice(40 * j + at, 40 * j + at + size)
+            keep_ref[at] = jnp.where(even, x, y)
+            send_ref[at] = jnp.where(even, y, x).astype(bf16)
+
+
+def merge_kernel(dp_ref, keep_own, keep_far, recv_own, recv_far, out_ref):
+    for i, (keep, recv) in enumerate(((keep_own, recv_own), (keep_far, recv_far))):
         for j in range(4):
-            m, n = slice(32 * j, 32 * j + 16), slice(32 * j + 16, 32 * j + 32)
-            u, b = up[128 + 8 * j : 136 + 8 * j], back[128 + 8 * j : 136 + 8 * j]
-            first = low(u.shape)
-            near = up[m], back[m], jnp.where(first, u, pltpu.roll(b, 4, 0))
-            far = up[n], back[n], jnp.where(first, pltpu.roll(u, 4, 0), b)
-            place((keep_h, keep_g), d, j, *(jnp.where(even, x, y) for x, y in zip(near, far)))
-            place((send_h, send_g), d, j, *(jnp.where(even, y, x) for x, y in zip(near, far)))
-
-
-def merge_kernel(keep_h, keep_g, recv_h, recv_g, out_ref):
-    for d in range(2):
-        for j in range(4):
-            own, got = take((keep_h, keep_g), d, j), take((recv_h, recv_g), d, j)
-            hid, grad, tail = ((a + b).astype(bf16) for a, b in zip(own, got))
-            out_ref[4 * d + j, 0:16] = hid
-            out_ref[4 * d + j, 16:32] = grad
-            out_ref[4 * d + j, 32:40] = tail
+            at = slice(40 * j, 40 * j + 40)
+            out_ref[4 * group(dp_ref, i) + j] = (keep[at] + recv[at].astype(f32)).astype(bf16)
 
 
 def split_kernel(full_ref, send_h, send_g):
     for d in range(2):
         for j in range(4):
             slab = full_ref.at[4 * d + j]
-            place((send_h, send_g), d, j, slab[0:16], slab[16:32], slab[32:40])
+            place(halves((send_h, send_g), d), d, j, slab[0:16], slab[16:32], slab[32:40])
 
 
 def gate(pre, back):
@@ -112,29 +116,29 @@
         out_ref[i, 32:40] = tail
 
 
-def ends_kernel(core_ref, side_ref, full_ref, recv_h, recv_g, up_ref, down_ref, hid_ref, grad_ref, keep_ref, send_ref):
+def ends_kernel(core_ref, side_ref, dp_ref, full_ref, recv_h, recv_g, up_ref, down_ref, hid_ref, grad_ref, keep_ref, send_ref):
     is_even = side_ref[0] == 0
     for d in range(2):
-        base = 160 * d
+        base = pl.multiple_of(160 * group(dp_ref, d), 32)
         hids, grads = [], []
         for j in range(4):
             slab = full_ref.at[4 * d + j]
             own = [slab[0:16].astype(f32), slab[16:32].astype(f32), slab[32:40].astype(f32)]
-            got = take((recv_h, recv_g), d, j)
+            got = take(halves((recv_h, recv_g), d), d, j)
             for k, (one, two) in enumerate(((own, got), (got, own))):
-                at = base + 32 * j + 16 * k
-                hid_ref[at : at + 16] = jnp.where(is_even, one[0], two[0]).astype(bf16)
-                grad_ref[at : at + 16] = jnp.where(is_even, one[1], two[1]).astype(bf16)
+                at = pl.ds(base + (32 * j + 16 * k), 16)
+                hid_ref[at] = jnp.where(is_even, one[0], two[0]).astype(bf16)
+                grad_ref[at] = jnp.where(is_even, one[1], two[1]).astype(bf16)
             even, odd = jnp.where(is_even, own[2], got[2]), jnp.where(is_even, got[2], own[2])
             first = low(even.shape)
             hids.append(jnp.where(first, even, pltpu.roll(odd, 4, 0)))
             grads.append(jnp.where(first, pltpu.roll(even, 4, 0), odd))
-        hid_ref[base + 128 : base + 160] = jnp.concatenate(hids).astype(bf16)
-        grad_ref[base + 128 : base + 160] = jnp.concatenate(grads).astype(bf16)
+        hid_ref[pl.ds(base + 128, 32)] = jnp.concatenate(hids).astype(bf16)
+        grad_ref[pl.ds(base + 128, 32)] = jnp.concatenate(grads).astype(bf16)
     near = core_ref[0] == 0
     pair = lax.broadcasted_iota(jnp.int32, (8, 128), 0) >> 1
     for d in range(2):
-        rows = slice(160 * d, 160 * d + 160)
+        rows = pl.ds(pl.multiple_of(160 * group(dp_ref, d), 32), 160)
         out = dot(hid_ref[rows], down_ref[...], ((1,), (0,)))
         inp = dot(grad_ref[rows], up_ref[...], ((1,), (1,)))
         for k in range(8):
@@ -180,31 +184,40 @@
     out_ref[...] = (keep_ref[...] + cores_ref[1 - core_ref[0]].astype(f32)).astype(bf16)
 
 
-def neighbours(to_up, to_down):
-    up = lax.ppermute(to_up, Y, [(i, (i + 1) % 8) for i in range(8)])
-    return up, lax.ppermute(to_down, Y, [(i, (i - 1) % 8) for i in range(8)])
+def neighbour(rows, step):
+    return lax.ppermute(rows, Y, [(i, (i + step) % 8) for i in range(8)])
 
 
 def body(tokens, cotangent, up_weight, down_weight):
-    core, side = lax.axis_index("c")[None], lax.axis_index("yl")[None]
+    core, side, dp = (lax.axis_index(n)[None] for n in ("c", "yl", "dp"))
     count, width = tokens.shape
     hid = up_weight.shape[1]
-    both = lax.all_gather(jnp.concatenate([tokens, cotangent]), "dp", axis=0, tiled=True)
-    both, core, side = lax.optimization_barrier((both, core, side))
-    wide, note = SDS((160, hid), f32), SDS((160, hid), bf16)
-    ordered = SDS((2 * count, width), bf16)
-    outs = (ordered, ordered, wide, wide, note, note)
-    acts, cots, *keep, to_up, to_down = call(partial_kernel, outs, side, both, up_weight, down_weight)
+    both = jnp.concatenate([tokens, cotangent])
+    both, core, side, dp = lax.optimization_barrier((both, core, side, dp))
+    far = lax.ppermute(both, "dp", [(0, 1), (1, 0)])
+    ordered = SDS((count, width), bf16)
+    acts, cots, keep, recv = [], [], [], []
+    for i, rows in enumerate((both, far)):
+        outs = ordered, ordered, SDS((160, hid), f32), SDS((160, hid), bf16)
+        ours, theirs, mine, sent = call(partial_kernel, outs, side, rows, up_weight, down_weight)
+        acts.append(ours)
+        cots.append(theirs)
+        keep.append(mine)
+        recv.append(neighbour(sent, 1 - 2 * i))
+    acts, cots = jnp.concatenate(acts), jnp.concatenate(cots)
+    note = SDS((160, hid), bf16)
     slabs = SDS((8, 40, hid), bf16)
-    parts = trade(call(merge_kernel, slabs, *keep, *neighbours(to_up, to_down)), PEERS)
+    parts = trade(call(merge_kernel, slabs, dp, *keep, *recv), PEERS)
     full = trade(call(activate_kernel, slabs, parts), PEERS)
-    others = neighbours(*call(split_kernel, (note, note), full))
+    to_up, to_down = call(split_kernel, (note, note), full)
+    others = neighbour(to_up, 1), neighbour(to_down, -1)
     rows = SDS((2 * count, hid), bf16)
     hidden, grad_pre, keep, send = call(
         ends_kernel,
         (rows, rows, SDS((16, 80, 128), f32), SDS((16, 80, 128), bf16)),
         core,
         side,
+        dp,
         full,
         *others,
         up_weight,

time: 115 us -> 111 us (0.965)
  the two profiles are of different devices: /device:TPU:8 before, /device:TPU:56 now
where the time goes in v5:
time: 111 us
  blocking collectives  47.5 us (43%)
  starting transfers between devices  27.7 us (25%)
  waiting for transfers between devices  23.6 us (21%)
  Pallas kernels  4.56 us (4%)
  matrix products  3.23 us (3%)
  local copies, waits for them, and re-layouts  2.36 us (2%)
    all_to_all x2, blocking collectives, trade(): return lax.all_to_all(parts, axis, 0, 0, tiled=True)  45.2 us
    ppermute x4, waiting for transfers between devices, neighbour(): return lax.ppermute(rows, Y, [(i, (i + step) % 8) for i in range(8)])  15.2 us
    ppermute x4, starting transfers between devices, neighbour(): return lax.ppermute(rows, Y, [(i, (i + step) % 8) for i in range(8)])  13.9 us
    all_to_all x1, starting transfers between devices, trade(): return lax.all_to_all(parts, axis, 0, 0, tiled=True)  10.4 us
    all_to_all x1, waiting for transfers between devices, trade(): return lax.all_to_all(parts, axis, 0, 0, tiled=True)  8.43 us
    pallas_call x8, Pallas kernels, call(): pl.pallas_call(kernel, out_shape=outs, in_specs=[pl.BlockSpec(memory_spac...  4.56 us
    ppermute x1, starting transfers between devices, body(): far = lax.ppermute(both, 'dp', [(0, 1), (1, 0)])  3.4 us
    dot_general x2, matrix products, dot(): return lax.dot_general(a, b, (dims, ((), ())), preferred_element_type=f32)  3.23 us
  transfers between devices with their start and end apart: 6, of which 5 were waited for; matrix products, arithmetic and copies ran while one was open for 3% of the time, Pallas kernels for 1%

profile of v5, /device:TPU:56, one launch (start us, length us, event | category | flops | bytes accessed | tf_op | source)
XLA Modules:
  0.0 110.8 jit_solution(17939889881863626192)
XLA Ops:
  0.6 1.0 pad_maximum_fusion.both_ref
  1.7 3.4 %collective-permute-start = (bf16[320,512]{1,0:T(8,128)(2,1)S(1)}, bf16[320,512]{1,0:T(8,128)(2,1)S(1)}, u32[]{:S(2)}, u32[]{:S(2)}) collective-permute-start(bf16[320,512]{1,0:T(8,128)(2,1)S(1)} %pad_maximum_fusion.both_ref), channel_id=1, source_target_pairs={{0,256},{256,0},{1,257},{257,1},{2,258},{258,2},{3,259},{259,3},{4... | collective-permute-start | bytes 983048 | tf_op jit(solution)/shard_map/ppermute | solution.py:197
  5.1 0.0 copy-start
  5.1 1.2 %copy-done = bf16[512,896]{1,0:T(8,128)(2,1)S(1)} copy-done((bf16[512,896]{1,0:T(8,128)(2,1)S(1)}, bf16[512,896]{1,0:T(8,128)(2,1)}, u32[]{:S(2)}) %copy-start) | copy-done | bytes 917528
  6.2 0.0 copy-start.2
  6.3 1.2 %copy-done.2 = bf16[896,512]{1,0:T(8,128)(2,1)S(1)} copy-done((bf16[896,512]{1,0:T(8,128)(2,1)S(1)}, bf16[896,512]{1,0:T(8,128)(2,1)}, u32[]{:S(2)}) %copy-start.2) | copy-done | bytes 917528
  7.4 0.0 copy-start.1
  7.4 0.0 copy-start.3
  7.4 0.8 shard_map.75
  8.2 5.6 %collective-permute-start.1 = (bf16[160,896]{1,0:T(8,128)(2,1)S(1)}, bf16[160,896]{1,0:T(8,128)(2,1)S(1)}, u32[]{:S(2)}, u32[]{:S(2)}) collective-permute-start(bf16[160,896]{1,0:T(8,128)(2,1)S(1)} %get-tuple-element.30), channel_id=1, source_target_pairs={{0,16},{16,32},{32,48},{48,64},{64,80},{80,96},{96,112},{112,0},{1... | collective-permute-start | bytes 860168 | tf_op jit(solution)/shard_map/ppermute | solution.py:188
  13.8 0.0 collective-permute-done.both_ref
  13.8 0.0 copy-done.1
  13.8 0.0 copy-done.3
  13.8 0.8 shard_map.76
  14.6 2.5 %collective-permute-start.2 = (bf16[160,896]{1,0:T(8,128)(2,1)S(1)}, bf16[160,896]{1,0:T(8,128)(2,1)S(1)}, u32[]{:S(2)}, u32[]{:S(2)}) collective-permute-start(bf16[160,896]{1,0:T(8,128)(2,1)S(1)} %get-tuple-element.31), channel_id=1, source_target_pairs={{0,112},{16,0},{32,16},{48,32},{64,48},{80,64},{96,80},{112,96},{1... | collective-permute-start | bytes 860168 | tf_op jit(solution)/shard_map/ppermute | solution.py:188
  17.0 1.3 %collective-permute-done.1.recv_own = bf16[160,896]{1,0:T(8,128)(2,1)S(1)} collective-permute-done((bf16[160,896]{1,0:T(8,128)(2,1)S(1)}, bf16[160,896]{1,0:T(8,128)(2,1)S(1)}, u32[]{:S(2)}, u32[]{:S(2)}) %collective-permute-start.1) | collective-permute-done | bytes 286752 | tf_op jit(solution)/shard_map/ppermute | solution.py:188
  18.4 6.2 %collective-permute-done.2.recv_far = bf16[160,896]{1,0:T(8,128)(2,1)S(1)} collective-permute-done((bf16[160,896]{1,0:T(8,128)(2,1)S(1)}, bf16[160,896]{1,0:T(8,128)(2,1)S(1)}, u32[]{:S(2)}, u32[]{:S(2)}) %collective-permute-start.2) | collective-permute-done | bytes 286752 | tf_op jit(solution)/shard_map/ppermute | solution.py:188
  24.6 0.1 shard_map.77
  24.7 20.4 %all_to_all.15.parts_ref = bf16[8,40,896]{2,1,0:T(8,128)(2,1)S(1)} all-to-all(bf16[8,40,896]{2,1,0:T(8,128)(2,1)S(1)} %shard_map.77), channel_id=1, replica_groups=mesh['dp'=2,'xh'=2,'yh'=4,'yl'=2,'z'=8,'c'=2] {'xh','yh'}, dimensions={0} | all-to-all | bytes 1146880 | tf_op jit(solution)/shard_map/all_to_all | solution.py:180
  45.1 0.1 shard_map.78
  45.3 24.8 %all_to_all.16.full_ref = bf16[8,40,896]{2,1,0:T(8,128)(2,1)S(1)} all-to-all(bf16[8,40,896]{2,1,0:T(8,128)(2,1)S(1)} %shard_map.78), channel_id=1, replica_groups=mesh['dp'=2,'xh'=2,'yh'=4,'yl'=2,'z'=8,'c'=2] {'xh','yh'}, dimensions={0} | all-to-all | bytes 1146880 | tf_op jit(solution)/shard_map/all_to_all | solution.py:180
  70.1 3.8 %collective-permute-start.3 = (bf16[160,896]{1,0:T(8,128)(2,1)S(1)}, bf16[160,896]{1,0:T(8,128)(2,1)S(1)}, u32[]{:S(2)}, u32[]{:S(2)}) collective-permute-start(bf16[160,896]{1,0:T(8,128)(2,1)S(1)} %get-tuple-element.32), channel_id=1, source_target_pairs={{0,16},{16,32},{32,48},{48,64},{64,80},{80,96},{96,112},{112,0},{1... | collective-permute-start | bytes 860168 | tf_op jit(solution)/shard_map/ppermute | solution.py:188
  73.9 2.1 %collective-permute-start.4 = (bf16[160,896]{1,0:T(8,128)(2,1)S(1)}, bf16[160,896]{1,0:T(8,128)(2,1)S(1)}, u32[]{:S(2)}, u32[]{:S(2)}) collective-permute-start(bf16[160,896]{1,0:T(8,128)(2,1)S(1)} %get-tuple-element.33), channel_id=1, source_target_pairs={{0,112},{16,0},{32,16},{48,32},{64,48},{80,64},{96,80},{112,96},{1... | collective-permute-start | bytes 860168 | tf_op jit(solution)/shard_map/ppermute | solution.py:188
  76.0 2.7 %collective-permute-done.3.recv_h = bf16[160,896]{1,0:T(8,128)(2,1)S(1)} collective-permute-done((bf16[160,896]{1,0:T(8,128)(2,1)S(1)}, bf16[160,896]{1,0:T(8,128)(2,1)S(1)}, u32[]{:S(2)}, u32[]{:S(2)}) %collective-permute-start.3) | collective-permute-done | bytes 286752 | tf_op jit(solution)/shard_map/ppermute | solution.py:188
  78.6 5.0 %collective-permute-done.4.recv_g = bf16[160,896]{1,0:T(8,128)(2,1)S(1)} collective-permute-done((bf16[160,896]{1,0:T(8,128)(2,1)S(1)}, bf16[160,896]{1,0:T(8,128)(2,1)S(1)}, u32[]{:S(2)}, u32[]{:S(2)}) %collective-permute-start.4) | collective-permute-done | bytes 286752 | tf_op jit(solution)/shard_map/ppermute | solution.py:188
  83.6 1.3 %shard_map.80 = (bf16[320,896]{1,0:T(8,128)(2,1)S(1)}, bf16[320,896]{1,0:T(8,128)(2,1)S(1)}, f32[16,80,128]{2,1,0:T(8,128)S(1)}, bf16[16,80,128]{2,1,0:T(8,128)(2,1)S(1)}) custom-call(s32[1]{0:T(128)} %bitcast.core_ref, s32[1]{0:T(128)} %bitcast.1.side_ref, s32[1]{0:T(128)} %bitcast.2.dp_ref, bf16[8,40,896]{2,1,0:T(8,128)(2,1)S(1)} %all_to_all.16.full_ref, ...), custom_call_target="tpu_custom_call" | custom-call | tf_op jit(solution)/shard_map/pallas_call | solution.py:18
  85.0 2.3 %all-gather = bf16[32,80,128]{2,1,0:T(8,128)(2,1)S(1)} all-gather(bf16[16,80,128]{2,1,0:T(8,128)(2,1)S(1)} %get-tuple-element.35), channel_id=2, replica_groups=mesh['dp'=2,'xh'=2,'yh'=4,'yl'=2,'z'=8,'c'=2] {'c'}, dimensions={0}, use_global_device_ids=true | all-gather | bytes 983040 | tf_op jit(solution)/shard_map/all_gather | solution.py:226
  87.2 0.8 shard_map.81
  88.0 10.4 %all-to-all-start.2 = ((bf16[16,80,128]{2,1,0:T(8,128)(2,1)}), bf16[16,80,128]{2,1,0:T(8,128)(2,1)S(1)}, u32[]{:S(2)}, u32[]{:S(2)}) async-start(bf16[16,80,128]{2,1,0:T(8,128)(2,1)} %shard_map.81), calls=%async_computation.2 | async-start | bytes 655360 | tf_op jit(solution)/shard_map/all_to_all | solution.py:180
  98.5 1.6 %convolution_convert_fusion.1 = bf16[512,896]{1,0:T(8,128)(2,1)} fusion(bf16[320,896]{1,0:T(8,128)(2,1)S(1)} %get-tuple-element.40, bf16[160,512]{1,0:T(8,128)(2,1)S(1)} %get-tuple-element.39, bf16[160,512]{1,0:T(8,128)(2,1)S(1)} %get-tuple-element.38), kind=kOutput, calls=%fused_computation.1 | convolution fusion | flops 294715392 | bytes 1818624 | tf_op jit(solution)/shard_map/dot_general | solution.py:14
  100.1 1.6 %convolution_convert_fusion = bf16[896,512]{1,0:T(8,128)(2,1)} fusion(bf16[320,896]{1,0:T(8,128)(2,1)S(1)} %get-tuple-element.41, bf16[160,512]{1,0:T(8,128)(2,1)S(1)} %get-tuple-element.43, bf16[160,512]{1,0:T(8,128)(2,1)S(1)} %get-tuple-element.42), kind=kOutput, calls=%fused_computation | convolution fusion | flops 294715392 | bytes 1818624 | tf_op jit(solution)/shard_map/dot_general | solution.py:14
  101.7 8.4 %all-to-all-done.2.parts_ref = bf16[16,80,128]{2,1,0:T(8,128)(2,1)S(1)} async-done(((bf16[16,80,128]{2,1,0:T(8,128)(2,1)}), bf16[16,80,128]{2,1,0:T(8,128)(2,1)S(1)}, u32[]{:S(2)}, u32[]{:S(2)}) %all-to-all-start.2) | async-done | bytes 327712 | tf_op jit(solution)/shard_map/all_to_all | solution.py:180
  110.1 0.7 shard_map.82
  (1 shorter events, 0.0 us)
Async XLA Ops:
  1.7 12.1 %collective-permute-start = (bf16[320,512]{1,0:T(8,128)(2,1)S(1)}, bf16[320,512]{1,0:T(8,128)(2,1)S(1)}, u32[]{:S(2)}, u32[]{:S(2)}) collective-permute-start(bf16[320,512]{1,0:T(8,128)(2,1)S(1)} %pad_maximum_fusion.both_ref), channel_id=1, source_target_pairs={{0,256},{256,0},{1,257},{257,1},{2,258},{258,2},{3,259},{259,3},{4... | collective-permute-start | bytes 983048 | tf_op jit(solution)/shard_map/ppermute | solution.py:197
  5.1 1.2 %copy-start = (bf16[512,896]{1,0:T(8,128)(2,1)S(1)}, bf16[512,896]{1,0:T(8,128)(2,1)}, u32[]{:S(2)}) copy-start(bf16[512,896]{1,0:T(8,128)(2,1)} %up_ref.5) | copy-start | bytes 2752516
  6.2 1.2 %copy-start.2 = (bf16[896,512]{1,0:T(8,128)(2,1)S(1)}, bf16[896,512]{1,0:T(8,128)(2,1)}, u32[]{:S(2)}) copy-start(bf16[896,512]{1,0:T(8,128)(2,1)} %down_ref.5) | copy-start | bytes 2752516
  7.4 6.4 %copy-start.1 = (bf16[512,896]{1,0:T(8,128)(2,1)S(1)}, bf16[512,896]{1,0:T(8,128)(2,1)}, u32[]{:S(2)}) copy-start(bf16[512,896]{1,0:T(8,128)(2,1)} %up_ref.5) | copy-start | bytes 2752516
  7.4 6.4 %copy-start.3 = (bf16[896,512]{1,0:T(8,128)(2,1)S(1)}, bf16[896,512]{1,0:T(8,128)(2,1)}, u32[]{:S(2)}) copy-start(bf16[896,512]{1,0:T(8,128)(2,1)} %down_ref.5) | copy-start | bytes 2752516
  8.2 10.2 %collective-permute-start.1 = (bf16[160,896]{1,0:T(8,128)(2,1)S(1)}, bf16[160,896]{1,0:T(8,128)(2,1)S(1)}, u32[]{:S(2)}, u32[]{:S(2)}) collective-permute-start(bf16[160,896]{1,0:T(8,128)(2,1)S(1)} %get-tuple-element.30), channel_id=1, source_target_pairs={{0,16},{16,32},{32,48},{48,64},{64,80},{80,96},{96,112},{112,0},{1... | collective-permute-start | bytes 860168 | tf_op jit(solution)/shard_map/ppermute | solution.py:188
  14.6 10.0 %collective-permute-start.2 = (bf16[160,896]{1,0:T(8,128)(2,1)S(1)}, bf16[160,896]{1,0:T(8,128)(2,1)S(1)}, u32[]{:S(2)}, u32[]{:S(2)}) collective-permute-start(bf16[160,896]{1,0:T(8,128)(2,1)S(1)} %get-tuple-element.31), channel_id=1, source_target_pairs={{0,112},{16,0},{32,16},{48,32},{64,48},{80,64},{96,80},{112,96},{1... | collective-permute-start | bytes 860168 | tf_op jit(solution)/shard_map/ppermute | solution.py:188
  70.1 8.5 %collective-permute-start.3 = (bf16[160,896]{1,0:T(8,128)(2,1)S(1)}, bf16[160,896]{1,0:T(8,128)(2,1)S(1)}, u32[]{:S(2)}, u32[]{:S(2)}) collective-permute-start(bf16[160,896]{1,0:T(8,128)(2,1)S(1)} %get-tuple-element.32), channel_id=1, source_target_pairs={{0,16},{16,32},{32,48},{48,64},{64,80},{80,96},{96,112},{112,0},{1... | collective-permute-start | bytes 860168 | tf_op jit(solution)/shard_map/ppermute | solution.py:188
  73.9 9.7 %collective-permute-start.4 = (bf16[160,896]{1,0:T(8,128)(2,1)S(1)}, bf16[160,896]{1,0:T(8,128)(2,1)S(1)}, u32[]{:S(2)}, u32[]{:S(2)}) collective-permute-start(bf16[160,896]{1,0:T(8,128)(2,1)S(1)} %get-tuple-element.33), channel_id=1, source_target_pairs={{0,112},{16,0},{32,16},{48,32},{64,48},{80,64},{96,80},{112,96},{1... | collective-permute-start | bytes 860168 | tf_op jit(solution)/shard_map/ppermute | solution.py:188
  88.0 22.1 %all-to-all-start.2 = ((bf16[16,80,128]{2,1,0:T(8,128)(2,1)}), bf16[16,80,128]{2,1,0:T(8,128)(2,1)S(1)}, u32[]{:S(2)}, u32[]{:S(2)}) async-start(bf16[16,80,128]{2,1,0:T(8,128)(2,1)} %shard_map.81), calls=%async_computation.2 | async-start | bytes 655360 | tf_op jit(solution)/shard_map/all_to_all | solution.py:180

commit v6 on v5

--- a/solution.py
+++ b/solution.py
@@ -5,7 +5,7 @@
 from jax.experimental.pallas import tpu as pltpu
 from jax.sharding import Mesh, PartitionSpec as P
 
-Y, PEERS, ROW = ("yh", "yl"), ("xh", "yh"), ("xh", "yh", "yl")
+Y, PEERS, ROW = ("yh", "yl"), ("yh", "xh"), ("xh", "yh", "yl")
 f32, bf16 = jnp.float32, jnp.bfloat16
 SDS = jax.ShapeDtypeStruct
 
@@ -85,13 +85,13 @@
     for i, (keep, recv) in enumerate(((keep_own, recv_own), (keep_far, recv_far))):
         for j in range(4):
             at = slice(40 * j, 40 * j + 40)
-            out_ref[4 * group(dp_ref, i) + j] = (keep[at] + recv[at].astype(f32)).astype(bf16)
+            out_ref[2 * j + group(dp_ref, i)] = (keep[at] + recv[at].astype(f32)).astype(bf16)
 
 
 def split_kernel(full_ref, send_h, send_g):
     for d in range(2):
         for j in range(4):
-            slab = full_ref.at[4 * d + j]
+            slab = full_ref.at[2 * j + d]
             place(halves((send_h, send_g), d), d, j, slab[0:16], slab[16:32], slab[32:40])
 
 
@@ -122,7 +122,7 @@
         base = pl.multiple_of(160 * group(dp_ref, d), 32)
         hids, grads = [], []
         for j in range(4):
-            slab = full_ref.at[4 * d + j]
+            slab = full_ref.at[2 * j + d]
             own = [slab[0:16].astype(f32), slab[16:32].astype(f32), slab[32:40].astype(f32)]
             got = take(halves((recv_h, recv_g), d), d, j)
             for k, (one, two) in enumerate(((own, got), (got, own))):
@@ -188,6 +188,11 @@
     return lax.ppermute(rows, Y, [(i, (i + step) % 8) for i in range(8)])
 
 
+def across(rows, first):
+    ways = [(y, c, (y + (1 if c == first else -1)) % 8) for y in range(8) for c in range(2)]
+    return lax.ppermute(rows, ("yh", "yl", "c"), [(2 * y + c, 2 * to + c) for y, c, to in ways])
+
+
 def body(tokens, cotangent, up_weight, down_weight):
     core, side, dp = (lax.axis_index(n)[None] for n in ("c", "yl", "dp"))
     count, width = tokens.shape
@@ -203,7 +208,7 @@
         acts.append(ours)
         cots.append(theirs)
         keep.append(mine)
-        recv.append(neighbour(sent, 1 - 2 * i))
+        recv.append(across(sent, i))
     acts, cots = jnp.concatenate(acts), jnp.concatenate(cots)
     note = SDS((160, hid), bf16)
     slabs = SDS((8, 40, hid), bf16)

time: 111 us -> 110 us (level)
    ppermute x4 -> x2, starting transfers between devices: 13.9 us -> 5.84 us  [neighbour(): return lax.ppermute(rows, Y, [(i, (i + step) % 8) for i in range(8)])]
    ppermute x0 -> x2, starting transfers between devices: none -> 8.03 us  [across(): lax.ppermute(rows, ('yh', 'yl', 'c'), [(2 * y + c, 2 * to + c) for y, c,...]
    ppermute x4 -> x2, waiting for transfers between devices: 15.2 us -> 7.33 us  [neighbour(): return lax.ppermute(rows, Y, [(i, (i + step) % 8) for i in range(8)])]
    ppermute x0 -> x2, waiting for transfers between devices: none -> 7.27 us  [across(): lax.ppermute(rows, ('yh', 'yl', 'c'), [(2 * y + c, 2 * to + c) for y, c,...]
where the time goes in v6:
time: 110 us
  blocking collectives  47.1 us (43%)
  starting transfers between devices  27.7 us (25%)
  waiting for transfers between devices  23 us (21%)
  Pallas kernels  4.56 us (4%)
  matrix products  3.23 us (3%)
  local copies, waits for them, and re-layouts  2.36 us (2%)
    all_to_all x2, blocking collectives, trade(): return lax.all_to_all(parts, axis, 0, 0, tiled=True)  44.8 us
    all_to_all x1, starting transfers between devices, trade(): return lax.all_to_all(parts, axis, 0, 0, tiled=True)  10.4 us
    all_to_all x1, waiting for transfers between devices, trade(): return lax.all_to_all(parts, axis, 0, 0, tiled=True)  8.43 us
    ppermute x2, starting transfers between devices, across(): lax.ppermute(rows, ('yh', 'yl', 'c'), [(2 * y + c, 2 * to + c) for y, c,...  8.03 us
    ppermute x2, waiting for transfers between devices, neighbour(): return lax.ppermute(rows, Y, [(i, (i + step) % 8) for i in range(8)])  7.33 us
    ppermute x2, waiting for transfers between devices, across(): lax.ppermute(rows, ('yh', 'yl', 'c'), [(2 * y + c, 2 * to + c) for y, c,...  7.27 us
    ppermute x2, starting transfers between devices, neighbour(): return lax.ppermute(rows, Y, [(i, (i + step) % 8) for i in range(8)])  5.84 us
    pallas_call x8, Pallas kernels, call(): pl.pallas_call(kernel, out_shape=outs, in_specs=[pl.BlockSpec(memory_spac...  4.56 us
  transfers between devices with their start and end apart: 6, of which 5 were waited for; matrix products, arithmetic and copies ran while one was open for 3% of the time, Pallas kernels for 1%

profile of v6, /device:TPU:56, one launch (start us, length us, event | category | flops | bytes accessed | tf_op | source)
XLA Modules:
  0.0 109.7 jit_solution(568862572104289504)
XLA Ops:
  0.6 1.0 pad_maximum_fusion.both_ref
  1.7 3.4 %collective-permute-start = (bf16[320,512]{1,0:T(8,128)(2,1)S(1)}, bf16[320,512]{1,0:T(8,128)(2,1)S(1)}, u32[]{:S(2)}, u32[]{:S(2)}) collective-permute-start(bf16[320,512]{1,0:T(8,128)(2,1)S(1)} %pad_maximum_fusion.both_ref), channel_id=1, source_target_pairs={{0,256},{256,0},{1,257},{257,1},{2,258},{258,2},{3,259},{259,3},{4... | collective-permute-start | bytes 983048 | tf_op jit(solution)/shard_map/ppermute | solution.py:202
  5.1 0.0 copy-start
  5.1 1.2 %copy-done = bf16[512,896]{1,0:T(8,128)(2,1)S(1)} copy-done((bf16[512,896]{1,0:T(8,128)(2,1)S(1)}, bf16[512,896]{1,0:T(8,128)(2,1)}, u32[]{:S(2)}) %copy-start) | copy-done | bytes 917528
  6.2 0.0 copy-start.2
  6.3 1.2 %copy-done.2 = bf16[896,512]{1,0:T(8,128)(2,1)S(1)} copy-done((bf16[896,512]{1,0:T(8,128)(2,1)S(1)}, bf16[896,512]{1,0:T(8,128)(2,1)}, u32[]{:S(2)}) %copy-start.2) | copy-done | bytes 917528
  7.4 0.0 copy-start.1
  7.4 0.0 copy-start.3
  7.4 0.8 shard_map.75
  8.2 5.6 %collective-permute-start.1 = (bf16[160,896]{1,0:T(8,128)(2,1)S(1)}, bf16[160,896]{1,0:T(8,128)(2,1)S(1)}, u32[]{:S(2)}, u32[]{:S(2)}) collective-permute-start(bf16[160,896]{1,0:T(8,128)(2,1)S(1)} %get-tuple-element.30), channel_id=1, source_target_pairs={{0,16},{1,113},{16,32},{17,1},{32,48},{33,17},{48,64},{49,33},{64,... | collective-permute-start | bytes 860168 | tf_op jit(solution)/shard_map/ppermute | solution.py:193
  13.8 0.0 collective-permute-done.both_ref
  13.8 0.0 copy-done.1
  13.8 0.0 copy-done.3
  13.8 0.8 shard_map.76
  14.6 2.5 %collective-permute-start.2 = (bf16[160,896]{1,0:T(8,128)(2,1)S(1)}, bf16[160,896]{1,0:T(8,128)(2,1)S(1)}, u32[]{:S(2)}, u32[]{:S(2)}) collective-permute-start(bf16[160,896]{1,0:T(8,128)(2,1)S(1)} %get-tuple-element.31), channel_id=1, source_target_pairs={{0,112},{1,17},{16,0},{17,33},{32,16},{33,49},{48,32},{49,65},{64,... | collective-permute-start | bytes 860168 | tf_op jit(solution)/shard_map/ppermute | solution.py:193
  17.0 3.4 %collective-permute-done.1.recv_own = bf16[160,896]{1,0:T(8,128)(2,1)S(1)} collective-permute-done((bf16[160,896]{1,0:T(8,128)(2,1)S(1)}, bf16[160,896]{1,0:T(8,128)(2,1)S(1)}, u32[]{:S(2)}, u32[]{:S(2)}) %collective-permute-start.1) | collective-permute-done | bytes 286752 | tf_op jit(solution)/shard_map/ppermute | solution.py:193
  20.4 3.9 %collective-permute-done.2.recv_far = bf16[160,896]{1,0:T(8,128)(2,1)S(1)} collective-permute-done((bf16[160,896]{1,0:T(8,128)(2,1)S(1)}, bf16[160,896]{1,0:T(8,128)(2,1)S(1)}, u32[]{:S(2)}, u32[]{:S(2)}) %collective-permute-start.2) | collective-permute-done | bytes 286752 | tf_op jit(solution)/shard_map/ppermute | solution.py:193
  24.3 0.1 shard_map.77
  24.4 18.3 %all_to_all.15.parts_ref = bf16[8,40,896]{2,1,0:T(8,128)(2,1)S(1)} all-to-all(bf16[8,40,896]{2,1,0:T(8,128)(2,1)S(1)} %shard_map.77), channel_id=1, replica_groups=mesh['dp'=2,'xh'=2,'yh'=4,'yl'=2,'z'=8,'c'=2] {'yh','xh'}, dimensions={0} | all-to-all | bytes 1146880 | tf_op jit(solution)/shard_map/all_to_all | solution.py:180
  42.7 0.1 shard_map.78
  42.8 26.5 %all_to_all.16.full_ref = bf16[8,40,896]{2,1,0:T(8,128)(2,1)S(1)} all-to-all(bf16[8,40,896]{2,1,0:T(8,128)(2,1)S(1)} %shard_map.78), channel_id=1, replica_groups=mesh['dp'=2,'xh'=2,'yh'=4,'yl'=2,'z'=8,'c'=2] {'yh','xh'}, dimensions={0} | all-to-all | bytes 1146880 | tf_op jit(solution)/shard_map/all_to_all | solution.py:180
  69.4 3.4 %collective-permute-start.3 = (bf16[160,896]{1,0:T(8,128)(2,1)S(1)}, bf16[160,896]{1,0:T(8,128)(2,1)S(1)}, u32[]{:S(2)}, u32[]{:S(2)}) collective-permute-start(bf16[160,896]{1,0:T(8,128)(2,1)S(1)} %get-tuple-element.32), channel_id=1, source_target_pairs={{0,16},{16,32},{32,48},{48,64},{64,80},{80,96},{96,112},{112,0},{1... | collective-permute-start | bytes 860168 | tf_op jit(solution)/shard_map/ppermute | solution.py:188
  72.8 2.4 %collective-permute-start.4 = (bf16[160,896]{1,0:T(8,128)(2,1)S(1)}, bf16[160,896]{1,0:T(8,128)(2,1)S(1)}, u32[]{:S(2)}, u32[]{:S(2)}) collective-permute-start(bf16[160,896]{1,0:T(8,128)(2,1)S(1)} %get-tuple-element.33), channel_id=1, source_target_pairs={{0,112},{16,0},{32,16},{48,32},{64,48},{80,64},{96,80},{112,96},{1... | collective-permute-start | bytes 860168 | tf_op jit(solution)/shard_map/ppermute | solution.py:188
  75.3 2.7 %collective-permute-done.3.recv_h = bf16[160,896]{1,0:T(8,128)(2,1)S(1)} collective-permute-done((bf16[160,896]{1,0:T(8,128)(2,1)S(1)}, bf16[160,896]{1,0:T(8,128)(2,1)S(1)}, u32[]{:S(2)}, u32[]{:S(2)}) %collective-permute-start.3) | collective-permute-done | bytes 286752 | tf_op jit(solution)/shard_map/ppermute | solution.py:188
  77.9 4.7 %collective-permute-done.4.recv_g = bf16[160,896]{1,0:T(8,128)(2,1)S(1)} collective-permute-done((bf16[160,896]{1,0:T(8,128)(2,1)S(1)}, bf16[160,896]{1,0:T(8,128)(2,1)S(1)}, u32[]{:S(2)}, u32[]{:S(2)}) %collective-permute-start.4) | collective-permute-done | bytes 286752 | tf_op jit(solution)/shard_map/ppermute | solution.py:188
  82.6 1.3 %shard_map.80 = (bf16[320,896]{1,0:T(8,128)(2,1)S(1)}, bf16[320,896]{1,0:T(8,128)(2,1)S(1)}, f32[16,80,128]{2,1,0:T(8,128)S(1)}, bf16[16,80,128]{2,1,0:T(8,128)(2,1)S(1)}) custom-call(s32[1]{0:T(128)} %bitcast.core_ref, s32[1]{0:T(128)} %bitcast.1.side_ref, s32[1]{0:T(128)} %bitcast.2.dp_ref, bf16[8,40,896]{2,1,0:T(8,128)(2,1)S(1)} %all_to_all.16.full_ref, ...), custom_call_target="tpu_custom_call" | custom-call | tf_op jit(solution)/shard_map/pallas_call | solution.py:18
  83.9 2.3 %all-gather = bf16[32,80,128]{2,1,0:T(8,128)(2,1)S(1)} all-gather(bf16[16,80,128]{2,1,0:T(8,128)(2,1)S(1)} %get-tuple-element.35), channel_id=2, replica_groups=mesh['dp'=2,'xh'=2,'yh'=4,'yl'=2,'z'=8,'c'=2] {'c'}, dimensions={0}, use_global_device_ids=true | all-gather | bytes 983040 | tf_op jit(solution)/shard_map/all_gather | solution.py:231
  86.2 0.8 shard_map.81
  87.0 10.4 %all-to-all-start.2 = ((bf16[16,80,128]{2,1,0:T(8,128)(2,1)}), bf16[16,80,128]{2,1,0:T(8,128)(2,1)S(1)}, u32[]{:S(2)}, u32[]{:S(2)}) async-start(bf16[16,80,128]{2,1,0:T(8,128)(2,1)} %shard_map.81), calls=%async_computation.2 | async-start | bytes 655360 | tf_op jit(solution)/shard_map/all_to_all | solution.py:180
  97.4 1.6 %convolution_convert_fusion.1 = bf16[512,896]{1,0:T(8,128)(2,1)} fusion(bf16[320,896]{1,0:T(8,128)(2,1)S(1)} %get-tuple-element.40, bf16[160,512]{1,0:T(8,128)(2,1)S(1)} %get-tuple-element.39, bf16[160,512]{1,0:T(8,128)(2,1)S(1)} %get-tuple-element.38), kind=kOutput, calls=%fused_computation.1 | convolution fusion | flops 294715392 | bytes 1818624 | tf_op jit(solution)/shard_map/dot_general | solution.py:14
  99.1 1.6 %convolution_convert_fusion = bf16[896,512]{1,0:T(8,128)(2,1)} fusion(bf16[320,896]{1,0:T(8,128)(2,1)S(1)} %get-tuple-element.41, bf16[160,512]{1,0:T(8,128)(2,1)S(1)} %get-tuple-element.43, bf16[160,512]{1,0:T(8,128)(2,1)S(1)} %get-tuple-element.42), kind=kOutput, calls=%fused_computation | convolution fusion | flops 294715392 | bytes 1818624 | tf_op jit(solution)/shard_map/dot_general | solution.py:14
  100.6 8.4 %all-to-all-done.2.parts_ref = bf16[16,80,128]{2,1,0:T(8,128)(2,1)S(1)} async-done(((bf16[16,80,128]{2,1,0:T(8,128)(2,1)}), bf16[16,80,128]{2,1,0:T(8,128)(2,1)S(1)}, u32[]{:S(2)}, u32[]{:S(2)}) %all-to-all-start.2) | async-done | bytes 327712 | tf_op jit(solution)/shard_map/all_to_all | solution.py:180
  109.1 0.7 shard_map.82
  (1 shorter events, 0.0 us)
Async XLA Ops:
  1.7 12.1 %collective-permute-start = (bf16[320,512]{1,0:T(8,128)(2,1)S(1)}, bf16[320,512]{1,0:T(8,128)(2,1)S(1)}, u32[]{:S(2)}, u32[]{:S(2)}) collective-permute-start(bf16[320,512]{1,0:T(8,128)(2,1)S(1)} %pad_maximum_fusion.both_ref), channel_id=1, source_target_pairs={{0,256},{256,0},{1,257},{257,1},{2,258},{258,2},{3,259},{259,3},{4... | collective-permute-start | bytes 983048 | tf_op jit(solution)/shard_map/ppermute | solution.py:202
  5.1 1.2 %copy-start = (bf16[512,896]{1,0:T(8,128)(2,1)S(1)}, bf16[512,896]{1,0:T(8,128)(2,1)}, u32[]{:S(2)}) copy-start(bf16[512,896]{1,0:T(8,128)(2,1)} %up_ref.5) | copy-start | bytes 2752516
  6.2 1.2 %copy-start.2 = (bf16[896,512]{1,0:T(8,128)(2,1)S(1)}, bf16[896,512]{1,0:T(8,128)(2,1)}, u32[]{:S(2)}) copy-start(bf16[896,512]{1,0:T(8,128)(2,1)} %down_ref.5) | copy-start | bytes 2752516
  7.4 6.4 %copy-start.1 = (bf16[512,896]{1,0:T(8,128)(2,1)S(1)}, bf16[512,896]{1,0:T(8,128)(2,1)}, u32[]{:S(2)}) copy-start(bf16[512,896]{1,0:T(8,128)(2,1)} %up_ref.5) | copy-start | bytes 2752516
  7.4 6.4 %copy-start.3 = (bf16[896,512]{1,0:T(8,128)(2,1)S(1)}, bf16[896,512]{1,0:T(8,128)(2,1)}, u32[]{:S(2)}) copy-start(bf16[896,512]{1,0:T(8,128)(2,1)} %down_ref.5) | copy-start | bytes 2752516
  8.2 12.2 %collective-permute-start.1 = (bf16[160,896]{1,0:T(8,128)(2,1)S(1)}, bf16[160,896]{1,0:T(8,128)(2,1)S(1)}, u32[]{:S(2)}, u32[]{:S(2)}) collective-permute-start(bf16[160,896]{1,0:T(8,128)(2,1)S(1)} %get-tuple-element.30), channel_id=1, source_target_pairs={{0,16},{1,113},{16,32},{17,1},{32,48},{33,17},{48,64},{49,33},{64,... | collective-permute-start | bytes 860168 | tf_op jit(solution)/shard_map/ppermute | solution.py:193
  14.6 9.7 %collective-permute-start.2 = (bf16[160,896]{1,0:T(8,128)(2,1)S(1)}, bf16[160,896]{1,0:T(8,128)(2,1)S(1)}, u32[]{:S(2)}, u32[]{:S(2)}) collective-permute-start(bf16[160,896]{1,0:T(8,128)(2,1)S(1)} %get-tuple-element.31), channel_id=1, source_target_pairs={{0,112},{1,17},{16,0},{17,33},{32,16},{33,49},{48,32},{49,65},{64,... | collective-permute-start | bytes 860168 | tf_op jit(solution)/shard_map/ppermute | solution.py:193
  69.4 8.5 %collective-permute-start.3 = (bf16[160,896]{1,0:T(8,128)(2,1)S(1)}, bf16[160,896]{1,0:T(8,128)(2,1)S(1)}, u32[]{:S(2)}, u32[]{:S(2)}) collective-permute-start(bf16[160,896]{1,0:T(8,128)(2,1)S(1)} %get-tuple-element.32), channel_id=1, source_target_pairs={{0,16},{16,32},{32,48},{48,64},{64,80},{80,96},{96,112},{112,0},{1... | collective-permute-start | bytes 860168 | tf_op jit(solution)/shard_map/ppermute | solution.py:188
  72.8 9.7 %collective-permute-start.4 = (bf16[160,896]{1,0:T(8,128)(2,1)S(1)}, bf16[160,896]{1,0:T(8,128)(2,1)S(1)}, u32[]{:S(2)}, u32[]{:S(2)}) collective-permute-start(bf16[160,896]{1,0:T(8,128)(2,1)S(1)} %get-tuple-element.33), channel_id=1, source_target_pairs={{0,112},{16,0},{32,16},{48,32},{64,48},{80,64},{96,80},{112,96},{1... | collective-permute-start | bytes 860168 | tf_op jit(solution)/shard_map/ppermute | solution.py:188
  87.0 22.1 %all-to-all-start.2 = ((bf16[16,80,128]{2,1,0:T(8,128)(2,1)}), bf16[16,80,128]{2,1,0:T(8,128)(2,1)S(1)}, u32[]{:S(2)}, u32[]{:S(2)}) async-start(bf16[16,80,128]{2,1,0:T(8,128)(2,1)} %shard_map.81), calls=%async_computation.2 | async-start | bytes 655360 | tf_op jit(solution)/shard_map/all_to_all | solution.py:180
